TPU v7x, 128 devices: a whole 4x4x4 slice. The times are simulated.
128 devices in a mesh: seq: 128 (over x, z, y, core).
Axes of the slice: x: 4, y: 4, z: 4, core: 2. Of those that a mesh axis runs over, the one named last changes fastest.
Arguments:
- queries: bfloat16 [131072, 4096], P('seq'), may hold values from -6 to 6
- span_keys: bfloat16 [131072, 1024], P('seq'), may hold values from -6 to 6
- span_values: bfloat16 [131072, 1024], P('seq'), may hold values from -6 to 6
- past_keys: bfloat16 [2, 128, 512, 1024], P(None, 'seq'), may hold values from -6 to 6
- past_values: bfloat16 [2, 128, 512, 1024], P(None, 'seq'), may hold values from -6 to 6
- selected: int32 [256, 8, 4], P('seq'), may hold values from 0 to 255, as said below
Outputs:
- attended: bfloat16 [131072, 4096], P('seq')
Inputs may be any that keep to these rules, and one draw needn't show every extreme that they name: `selected`: query blocks k * 2 to (k + 1) * 2 - 1 form group k. Among the 64 numbers of one group, at most 1 are equal modulo 128, and some residue is named exactly 1 times.
All inputs are finite; a program needn't handle non-finite values.
Results may differ from a plain program's by a relative error of at most 0.005.
Values may be sent and summed in bfloat16 or wider, within the bound.
No kernel may reach another device: no remote copies, remote signals or barrier semaphores. Data moves between devices by JAX's collectives and lax.ppermute only.
A program may use at most 256 MiB of HBM per device.

v0:
```python
import jax
import jax.numpy as jnp
from jax import lax
from jax.sharding import PartitionSpec as P


def attend_head(query_head, far_keys, far_values, near_keys, near_values, causal):
    scale = query_head.shape[-1] ** (-0.5)
    far = (
        jnp.einsum("igd,kd->gik", query_head, far_keys, preferred_element_type=jnp.float32) * scale
    )
    near = (
        jnp.einsum("igd,jd->gij", query_head, near_keys, preferred_element_type=jnp.float32) * scale
    )
    near = jnp.where(causal, near, -jnp.inf)
    top = jnp.maximum(jnp.max(far, axis=-1), jnp.max(near, axis=-1))[..., None]
    far_weight = jnp.exp(far - top)
    near_weight = jnp.exp(near - top)
    total = jnp.sum(far_weight, axis=-1, keepdims=True) + jnp.sum(
        near_weight, axis=-1, keepdims=True
    )
    far_probs = (far_weight / total).astype(jnp.bfloat16)
    near_probs = (near_weight / total).astype(jnp.bfloat16)
    result = jnp.einsum("gik,kd->igd", far_probs, far_values, preferred_element_type=jnp.float32)
    result = result + jnp.einsum(
        "gij,jd->igd", near_probs, near_values, preferred_element_type=jnp.float32
    )
    return result.astype(jnp.bfloat16)


def owner_ranks(owners):
    length = owners.shape[-1]
    later = lax.broadcasted_iota(jnp.int32, (length, length), 0)
    sooner = lax.broadcasted_iota(jnp.int32, (length, length), 1)
    same = owners[..., :, None] == owners[..., None, :]
    return jnp.sum(jnp.where(same & (sooner < later), 1, 0), axis=-1).astype(jnp.int32)


def shards(queries, span_keys, span_values, past_keys, past_values, selected):
    count = lax.axis_size("seq")
    local_blocks = selected.shape[0]
    heads = selected.shape[1]
    picks = selected.shape[2]
    needed = local_blocks * heads * picks
    slots = (needed + count - 1) // count
    block = queries.shape[0] // local_blocks
    width = past_keys.shape[-1] // heads
    group = queries.shape[1] // (heads * width)
    chosen = selected.reshape(-1)
    owners = chosen % count
    ranks = owner_ranks(owners)
    head_flat = lax.broadcasted_iota(jnp.int32, selected.shape, 1).reshape(-1)
    wanted = chosen // count * heads + head_flat + 1
    slot_ids = owners * slots + ranks
    match = slot_ids[None, :] == jnp.arange(count * slots, dtype=jnp.int32)[:, None]
    outgoing = jnp.sum(jnp.where(match, wanted[None, :], 0), axis=1).reshape(count, slots)
    incoming = lax.all_to_all(outgoing, "seq", split_axis=0, concat_axis=0, tiled=True) - 1
    request = incoming.reshape(-1)
    usable = (request >= 0)[:, None, None]
    request = jnp.maximum(request, 0)
    local_block = request // heads
    local_head = request % heads
    keys_local = past_keys.reshape(past_keys.shape[0], block, heads, width)
    values_local = past_values.reshape(past_values.shape[0], block, heads, width)
    send_keys = jnp.where(
        usable, keys_local[local_block, :, local_head, :], jnp.zeros((), jnp.bfloat16)
    ).reshape(count, slots, block, width)
    send_values = jnp.where(
        usable, values_local[local_block, :, local_head, :], jnp.zeros((), jnp.bfloat16)
    ).reshape(count, slots, block, width)
    arrived_keys, arrived_values = (
        lax.all_to_all(send_keys, "seq", split_axis=0, concat_axis=0, tiled=True),
        lax.all_to_all(send_values, "seq", split_axis=0, concat_axis=0, tiled=True),
    )
    far_keys = arrived_keys[owners, ranks].reshape(local_blocks * heads, picks * block, width)
    far_values = arrived_values[owners, ranks].reshape(local_blocks * heads, picks * block, width)
    query_heads = (
        queries.reshape(local_blocks, block, heads, group, width)
        .transpose(0, 2, 1, 3, 4)
        .reshape(local_blocks * heads, block, group, width)
    )
    near_keys = (
        span_keys.reshape(local_blocks, block, heads, width)
        .transpose(0, 2, 1, 3)
        .reshape(local_blocks * heads, block, width)
    )
    near_values = (
        span_values.reshape(local_blocks, block, heads, width)
        .transpose(0, 2, 1, 3)
        .reshape(local_blocks * heads, block, width)
    )
    causal = lax.broadcasted_iota(jnp.int32, (block, block), 1) <= lax.broadcasted_iota(
        jnp.int32, (block, block), 0
    )
    results = lax.map(
        lambda items: attend_head(items[0], items[1], items[2], items[3], items[4], causal),
        (query_heads, far_keys, far_values, near_keys, near_values),
    )
    results = results.reshape(local_blocks, heads, block, group, width).transpose(0, 2, 1, 3, 4)
    return results.reshape(local_blocks * block, heads * group * width)


def solution(mesh):
    return jax.shard_map(
        shards,
        mesh=mesh,
        in_specs=(
            P("seq", None),
            P("seq", None),
            P("seq", None),
            P(None, "seq", None, None),
            P(None, "seq", None, None),
            P("seq", None, None),
        ),
        out_specs=P("seq", None),
        check_vma=False,
    )
```

profile of v0, /device:TPU:1, one launch (start us, length us, event | category | flops | bytes accessed | tf_op | source)
XLA Modules:
  0.0 1069.9 jit_solution(11230892312594722302)
XLA Ops:
  2.0 11.5 %all-to-all-start = ((s32[128,1,1]{2,1,0:T(1,128)}), s32[128,1,1]{2,1,0:T(1,128)S(1)}, u32[]{:S(2)}, u32[]{:S(2)}) async-start(s32[128,1,1]{2,1,0:T(1,128)} %copy.76), calls=%async_computation | async-start | bytes 131072 | tf_op jit(solution)/shard_map/all_to_all | solution.py:57
  37.7 8.4 gather_fusion
  46.1 10.1 gather_fusion.2
  56.2 17.6 %fusion.33 = (bf16[128,1,512,128]{3,2,1,0:T(8,128)(2,1)S(1)}, bf16[128,1,512,128]{3,2,1,0:T(8,128)(2,1)}) fusion(bf16[128,512,128]{2,1,0:T(8,128)(2,1)} %gather_fusion.2, pred[128]{0:T(512)(128)(4,1)S(1)} %get-tuple-element.121, bf16[128,512,128]{2,1,0:T(8,128)(2,1)} %gather_fusion), kind=kLoop, calls=%fused_computation.44 | loop fusion | flops 16777216 | bytes 67108992 | tf_op jit(solution)/shard_map/jit(_where)/select_n | solution.py:65
  73.9 198.8 %all_to_all.19 = bf16[128,1,512,128]{3,2,1,0:T(8,128)(2,1)} all-to-all(bf16[128,1,512,128]{3,2,1,0:T(8,128)(2,1)S(1)} %get-tuple-element.122), channel_id=1, replica_groups=mesh['seq'=128] {'seq'}, dimensions={0} | all-to-all | bytes 33554432 | tf_op jit(solution)/shard_map/all_to_all | solution.py:72
  272.7 14.6 %all-to-all-start.1 = ((bf16[128,1,512,128]{3,2,1,0:T(8,128)(2,1)}), bf16[128,1,512,128]{3,2,1,0:T(8,128)(2,1)}, u32[]{:S(2)}, u32[]{:S(2)}) async-start(bf16[128,1,512,128]{3,2,1,0:T(8,128)(2,1)} %get-tuple-element.123), calls=%async_computation.1 | async-start | bytes 33554432 | tf_op jit(solution)/shard_map/all_to_all | solution.py:73
  287.4 14.3 %reshape.318 = bf16[2,512,8,4,128]{4,3,2,1,0:T(4,128)(2,1)} reshape(bf16[1024,4096]{1,0:T(8,128)(2,1)} %param.8) | data formatting | bytes 16777216 | tf_op jit(solution)/shard_map/reshape | solution.py:78
  301.7 10.0 copy.84
  317.3 11.3 %gather_fusion.3 = bf16[64,512,128]{2,1,0:T(8,128)(2,1)} fusion(bf16[128,1,512,128]{3,2,1,0:T(8,128)(2,1)} %all_to_all.19, s32[64]{0:T(128)S(1)} %fusion.48), kind=kCustom, calls=%fused_computation.3 | custom fusion | bytes 16777728 | tf_op jit(solution)/shard_map/gather | solution.py:75
  328.7 191.1 %all-to-all-done.1 = bf16[128,1,512,128]{3,2,1,0:T(8,128)(2,1)} async-done(((bf16[128,1,512,128]{3,2,1,0:T(8,128)(2,1)}), bf16[128,1,512,128]{3,2,1,0:T(8,128)(2,1)}, u32[]{:S(2)}, u32[]{:S(2)}) %all-to-all-start.1) | async-done | bytes 16777248 | tf_op jit(solution)/shard_map/all_to_all | solution.py:73
  519.7 11.4 %gather_fusion.1 = bf16[64,512,128]{2,1,0:T(8,128)(2,1)} fusion(bf16[128,1,512,128]{3,2,1,0:T(8,128)(2,1)} %all-to-all-done.1, s32[64]{0:T(128)S(1)} %fusion.48), kind=kCustom, calls=%fused_computation.1 | custom fusion | bytes 16777728 | tf_op jit(solution)/shard_map/gather | solution.py:76
  531.1 509.8 %while.11 = (s32[]{:T(128)}, bf16[16,512,4,128]{1,3,2,0:T(8,128)(2,1)}, bf16[16,2048,128]{2,1,0:T(8,128)(2,1)}, bf16[16,2048,128]{2,1,0:T(8,128)(2,1)}, bf16[16,...) while((s32[]{:T(128)}, ...), condition=%wide.region_7.8_spmd.clone, body=%wide.region_2.7_spmd.clone.sunk | while | flops 2735468544 | bytes 69078616 | solution.py:95
  533.1 9.3 bitcast_reduce_fusion.2
  543.3 8.5 fusion.60
  565.0 9.3 bitcast_reduce_fusion.2
  575.2 8.5 fusion.60
  596.9 9.3 bitcast_reduce_fusion.2
  607.0 8.5 fusion.60
  628.7 9.3 bitcast_reduce_fusion.2
  638.9 8.5 fusion.60
  647.4 7.9 fusion.62
  660.6 9.3 bitcast_reduce_fusion.2
  670.8 8.5 fusion.60
  679.3 7.9 fusion.62
  692.5 9.3 bitcast_reduce_fusion.2
  702.6 8.5 fusion.60
  724.3 9.3 bitcast_reduce_fusion.2
  734.5 8.5 fusion.60
  756.2 9.3 bitcast_reduce_fusion.2
  766.4 8.5 fusion.60
  788.1 9.3 bitcast_reduce_fusion.2
  798.2 8.5 fusion.60
  819.9 9.3 bitcast_reduce_fusion.2
  830.1 8.5 fusion.60
  851.8 9.3 bitcast_reduce_fusion.2
  862.0 8.5 fusion.60
  883.7 9.3 bitcast_reduce_fusion.2
  893.8 8.5 fusion.60
  915.5 9.3 bitcast_reduce_fusion.2
  925.7 8.5 fusion.60
  947.4 9.3 bitcast_reduce_fusion.2
  957.6 8.5 fusion.60
  979.3 9.3 bitcast_reduce_fusion.2
  989.4 8.5 fusion.60
  1011.1 9.3 bitcast_reduce_fusion.2
  1021.3 8.5 fusion.60
  1040.9 14.6 %copy.88 = bf16[2,8,512,4,128]{4,3,1,2,0:T(4,128)(2,1)} copy(bf16[2,8,512,4,128]{2,4,3,1,0:T(8,128)(2,1)} %bitcast.153) | data formatting | bytes 16777216 | tf_op jit(solution)/shard_map/reshape | solution.py:99
  1055.5 14.4 %reshape.325 = bf16[1024,4096]{1,0:T(8,128)(2,1)} reshape(bf16[2,512,8,4,128]{4,3,2,1,0:T(4,128)(2,1)} %bitcast.149) | data formatting | bytes 16777216 | tf_op jit(solution)/shard_map/reshape | solution.py:100
  (138 shorter events, 241.4 us)
Async XLA Ops:
  2.0 26.4 %all-to-all-start = ((s32[128,1,1]{2,1,0:T(1,128)}), s32[128,1,1]{2,1,0:T(1,128)S(1)}, u32[]{:S(2)}, u32[]{:S(2)}) async-start(s32[128,1,1]{2,1,0:T(1,128)} %copy.76), calls=%async_computation | async-start | bytes 131072 | tf_op jit(solution)/shard_map/all_to_all | solution.py:57
  272.7 247.0 %all-to-all-start.1 = ((bf16[128,1,512,128]{3,2,1,0:T(8,128)(2,1)}), bf16[128,1,512,128]{3,2,1,0:T(8,128)(2,1)}, u32[]{:S(2)}, u32[]{:S(2)}) async-start(bf16[128,1,512,128]{3,2,1,0:T(8,128)(2,1)} %get-tuple-element.123), calls=%async_computation.1 | async-start | bytes 33554432 | tf_op jit(solution)/shard_map/all_to_all | solution.py:73
  301.7 10.0 copy-start
  311.7 2.4 copy-start.1
where the time goes:
time: 1080 us; the launch traced here: 1070 us
  matrix products  357 us (33%)
  blocking collectives  199 us (18%)
  waiting for transfers between devices  191 us (18%)
  other arithmetic  179 us (17%)
  local copies, waits for them, and re-layouts  117 us (11%)
  starting transfers between devices  26.1 us (2%)
    all_to_all x1, blocking collectives, shards(): lax.all_to_all(send_keys, 'seq', split_axis=0, concat_axis=0, tiled=True)  199 us
    all_to_all x1, waiting for transfers between devices, shards(): lax.all_to_all(send_values, 'seq', split_axis=0, concat_axis=0, tiled=True)  191 us
    dot_general x16, matrix products, attend_head(): jnp.einsum('igd,kd->gik', query_head, far_keys, preferred_element_type=jn...  148 us
    reduce_sum x16, other arithmetic, attend_head(): jnp.sum(far_weight, axis=-1, keepdims=True)  136 us
    dot_general x16, matrix products, attend_head(): jnp.einsum('gik,kd->igd', far_probs, far_values, preferred_element_type=j...  127 us
    dot_general x16, matrix products, attend_head(): jnp.einsum('gij,jd->igd', near_probs, near_values, preferred_element_type...  51.4 us
    dot_general x16, matrix products, attend_head(): jnp.einsum('igd,jd->gij', query_head, near_keys, preferred_element_type=j...  31.4 us
    reshape x2, local copies, waits for them, and re-layouts, shards(): queries.reshape(local_blocks, block, heads, group, width)  24.3 us
  transfers between devices with their start and end apart: 2, of which 1 were waited for; matrix products, arithmetic and copies ran while one was open for 5% of the time, Pallas kernels for 0%

commit v1 on v0

v1 whole, which is shorter than its diff:
```python
import functools
import jax
import jax.numpy as jnp
from jax import lax
from jax.experimental import pallas as pl
from jax.experimental.pallas import tpu as pltpu
from jax.sharding import PartitionSpec as P

BLOCK, HD, GROUP, TOPK = 512, 128, 4, 4
SHIFT = 1024


def segments(start, rows):
    out = []
    if start < BLOCK:
        n = min(rows, BLOCK - start)
        out.append((0, n, 0, start))
        if rows > n:
            out.append((n, rows - n, 1, 0))
    else:
        out.append((0, rows, 1, start - BLOCK))
    return out


def attend_kernel(pieces, counts, table, q_ref, nk_ref, nv_ref, *refs):
    total = sum(counts)
    sources = refs[:total]
    out_ref, k_buf, v_buf, nv_buf, sems = refs[total:]
    step = pl.program_id(0)
    steps = pl.num_programs(0)
    scale = HD ** -0.5 * 1.4426950408889634

    def fetch(g, slot):
        for j in range(TOPK):
            base = 0
            for p, (start, rows) in enumerate(pieces):
                where = table[p, g * TOPK + j]
                which = where // SHIFT
                row = where - which * SHIFT
                for n in range(counts[p]):
                    def go(ref=sources[base + n]):
                        for s0, length, kind, d0 in segments(start, rows):
                            if kind == 0:
                                dst = k_buf.at[slot, j, pl.ds(d0, length), :]
                            else:
                                dst = v_buf.at[slot, j, pl.ds(d0, length), pl.ds(0, HD)]
                            pltpu.make_async_copy(
                                ref.at[row, pl.ds(s0, length), :], dst, sems.at[slot]
                            ).start()
                    if counts[p] == 1:
                        go()
                    else:
                        pl.when(which == n)(go)
                base += counts[p]

    slot = lax.rem(step, 2)

    @pl.when(step == 0)
    def _():
        v_buf[:, :, :, HD:] = jnp.ones((2, TOPK, BLOCK, HD), jnp.bfloat16)
        nv_buf[:, HD:] = jnp.ones((BLOCK, HD), jnp.bfloat16)
        fetch(0, 0)

    @pl.when(step + 1 < steps)
    def _():
        fetch(step + 1, 1 - slot)

    nv_buf[:, :HD] = nv_ref[...]
    pltpu.make_async_copy(k_buf.at[slot], k_buf.at[slot], sems.at[slot]).wait()
    pltpu.make_async_copy(
        k_buf.at[slot], v_buf.at[slot, :, :, pl.ds(0, HD)], sems.at[slot]
    ).wait()

    half = 256
    for a in range(GROUP):
        for part in range(2):
            keys = half * (part + 1)
            q = q_ref[pl.ds(part * half, half), pl.ds(a * HD, HD)]
            dims = (((1,), (1,)), ((), ()))
            scores = [
                lax.dot_general(q, k_buf[slot, j], dims, preferred_element_type=jnp.float32)
                for j in range(TOPK)
            ]
            near = lax.dot_general(q, nk_ref[:keys, :], dims, preferred_element_type=jnp.float32)
            seen = lax.broadcasted_iota(jnp.int32, (half, keys), 1) <= (
                lax.broadcasted_iota(jnp.int32, (half, keys), 0) + part * half
            )
            near = jnp.where(seen, near, -jnp.inf)
            top = jnp.max(near, axis=1, keepdims=True)
            for s in scores:
                top = jnp.maximum(top, jnp.max(s, axis=1, keepdims=True))
            top = top * scale
            acc = jnp.dot(
                jnp.exp2(near * scale - top).astype(jnp.bfloat16),
                nv_buf[:keys, :],
                preferred_element_type=jnp.float32,
            )
            for j in range(TOPK):
                acc += jnp.dot(
                    jnp.exp2(scores[j] * scale - top).astype(jnp.bfloat16),
                    v_buf[slot, j],
                    preferred_element_type=jnp.float32,
                )
            out_ref[pl.ds(part * half, half), pl.ds(a * HD, HD)] = (
                acc[:, :HD] / acc[:, HD:]
            ).astype(jnp.bfloat16)


def attend(queries, span_keys, span_values, table, pieces, groups):
    tokens, width = queries.shape
    heads = span_keys.shape[1] // HD
    blocks = tokens // BLOCK
    counts = [len(g) for g in groups]
    flat = [s for g in groups for s in g]
    steps = blocks * heads
    place = lambda g, t: (g // heads, lax.rem(g, heads))
    keys = BLOCK * (TOPK + 1)
    return pl.pallas_call(
        functools.partial(attend_kernel, pieces, counts),
        out_shape=jax.ShapeDtypeStruct((tokens, width), jnp.bfloat16),
        grid_spec=pltpu.PrefetchScalarGridSpec(
            num_scalar_prefetch=1,
            grid=(steps,),
            in_specs=[
                pl.BlockSpec((BLOCK, GROUP * HD), place),
                pl.BlockSpec((BLOCK, HD), place),
                pl.BlockSpec((BLOCK, HD), place),
            ]
            + [pl.BlockSpec(memory_space=pl.ANY)] * len(flat),
            out_specs=pl.BlockSpec((BLOCK, GROUP * HD), place),
            scratch_shapes=[
                pltpu.VMEM((2, TOPK, BLOCK, HD), jnp.bfloat16),
                pltpu.VMEM((2, TOPK, BLOCK, 2 * HD), jnp.bfloat16),
                pltpu.VMEM((BLOCK, 2 * HD), jnp.bfloat16),
                pltpu.SemaphoreType.DMA((2,)),
            ],
        ),
        compiler_params=pltpu.CompilerParams(
            dimension_semantics=("arbitrary",), vmem_limit_bytes=48 * 1024 * 1024
        ),
        cost_estimate=pl.CostEstimate(
            flops=4 * tokens * width * keys,
            transcendentals=tokens * (width // HD) * keys,
            bytes_accessed=50 * 1024 * 1024,
        ),
        name="attend",
    )(table, queries, span_keys, span_values, *flat)


def shards(queries, span_keys, span_values, past_keys, past_values, selected):
    count = lax.axis_size("seq")
    heads = selected.shape[1]
    chosen = selected.reshape(-1)
    owners = chosen % count
    head_flat = lax.broadcasted_iota(jnp.int32, selected.shape, 1).reshape(-1)
    wanted = chosen // count * heads + head_flat + 1
    match = owners[None, :] == jnp.arange(count, dtype=jnp.int32)[:, None]
    outgoing = jnp.sum(jnp.where(match, wanted[None, :], 0), axis=1).reshape(count, 1)
    incoming = lax.all_to_all(outgoing, "seq", split_axis=0, concat_axis=0, tiled=True)
    item = jnp.maximum(incoming.reshape(-1) - 1, 0)
    stacked = jnp.concatenate(
        [
            x.reshape(-1, BLOCK, heads, HD).transpose(0, 2, 1, 3).reshape(-1, BLOCK, HD)
            for x in (past_keys, past_values)
        ],
        axis=1,
    )
    arrived = lax.all_to_all(stacked[item], "seq", split_axis=0, concat_axis=0, tiled=True)
    return attend(
        queries, span_keys, span_values, owners[None, :], [(0, 2 * BLOCK)], [[arrived]]
    )


def solution(mesh):
    return jax.shard_map(
        shards,
        mesh=mesh,
        in_specs=(
            P("seq", None),
            P("seq", None),
            P("seq", None),
            P(None, "seq", None, None),
            P(None, "seq", None, None),
            P("seq", None, None),
        ),
        out_specs=P("seq", None),
        check_vma=False,
    )
```

time: 1080 us -> 713 us (0.66)
  the two profiles are of different devices: /device:TPU:1 before, /device:TPU:122 now
where the time goes in v1:
time: 713 us
  waiting for transfers between devices  534 us (75%)
  Pallas kernels  123 us (17%)
  local copies, waits for them, and re-layouts  28.7 us (4%)
  starting transfers between devices  20 us (3%)
    all_to_all x1, waiting for transfers between devices, shards(): lax.all_to_all(stacked[item], 'seq', split_axis=0, concat_axis=0, tiled=T...  534 us
    pallas_call x1, Pallas kernels, attend(): pl.pallas_call(functools.partial(attend_kernel, pieces, counts), out_shap...  123 us
    gather x1, local copies, waits for them, and re-layouts, shards(): stacked[item]  14.8 us
  transfers between devices with their start and end apart: 2, of which 1 were waited for; matrix products, arithmetic and copies ran while one was open for 2% of the time, Pallas kernels for 0%

profile of v1, /device:TPU:122, one launch (start us, length us, event | category | flops | bytes accessed | tf_op | source)
XLA Modules:
  0.0 712.7 jit_solution(10160465593368679948)
XLA Ops:
  0.0 0.8 copy.31
  0.8 0.1 reshape.136
  0.9 0.1 reshape.137
  1.0 0.1 select_reduce_fusion
  1.1 0.8 copy.37
  1.8 9.7 %all-to-all-start = ((s32[128,1,1]{2,1,0:T(1,128)}), s32[128,1,1]{2,1,0:T(1,128)S(1)}, u32[]{:S(2)}, u32[]{:S(2)}) async-start(s32[128,1,1]{2,1,0:T(1,128)} %copy.37), calls=%async_computation | async-start | bytes 131072 | tf_op jit(solution)/shard_map/all_to_all | solution.py:159
  11.5 2.9 copy.32
  14.4 2.4 copy.33
  16.8 2.9 copy.34
  19.6 2.4 copy.35
  22.0 4.6 pad_maximum_fusion
  26.7 0.0 all-to-all-done
  26.7 2.4 maximum_reduce_fusion
  29.0 14.8 %gather_fusion = bf16[128,1024,128]{2,1,0:T(8,128)(2,1)} fusion(bf16[16,1024,128]{2,1,0:T(8,128)(2,1)} %pad_maximum_fusion, s32[1024]{0:T(1024)S(1)} %pad_clamp_fusion), kind=kCustom, calls=%fused_computation | custom fusion | bytes 67109376 | tf_op jit(solution)/shard_map/gather | solution.py:168
  43.9 0.0 copy-start
  43.9 10.3 %all-to-all-start.1 = ((bf16[128,1024,128]{2,1,0:T(8,128)(2,1)}), bf16[128,1024,128]{2,1,0:T(8,128)(2,1)}, u32[]{:S(2)}, u32[]{:S(2)}) async-start(bf16[128,1024,128]{2,1,0:T(8,128)(2,1)} %gather_fusion), calls=%async_computation.1 | async-start | bytes 67108864 | tf_op jit(solution)/shard_map/all_to_all | solution.py:168
  54.2 0.1 reshape.131
  54.3 533.6 %all-to-all-done.1.refs_0_ = bf16[128,1024,128]{2,1,0:T(8,128)(2,1)} async-done(((bf16[128,1024,128]{2,1,0:T(8,128)(2,1)}), bf16[128,1024,128]{2,1,0:T(8,128)(2,1)}, u32[]{:S(2)}, u32[]{:S(2)}) %all-to-all-start.1) | async-done | bytes 33554464 | tf_op jit(solution)/shard_map/all_to_all | solution.py:168
  587.8 0.0 copy-done
  587.8 0.0 copy-start.1
  587.8 1.6 copy-done.1
  589.4 123.1 %attend.1 = bf16[1024,4096]{1,0:T(8,128)(2,1)} custom-call(s32[1,64]{1,0:T(1,128)S(1)} %and_select_fusion.2.table, bf16[1024,4096]{1,0:T(8,128)(2,1)} %q_ref.1, bf16[1024,1024]{1,0:T(8,128)(2,1)S(1)} %copy-done, bf16[1024,1024]{1,0:T(8,128)(2,1)S(1)} %copy-done.1, bf16[128,1024,128]{2,1,0:T(8,128)(2,1)} %all-to-all-done.1.refs_0_), custom_call_target="tpu_custom_call" | custom-call | flops 42949672960 | bytes 52428800 | tf_op jit(solution)/shard_map/attend/pallas_call | solution.py:118
  (4 shorter events, 0.0 us)
Async XLA Ops:
  1.8 24.8 %all-to-all-start = ((s32[128,1,1]{2,1,0:T(1,128)}), s32[128,1,1]{2,1,0:T(1,128)S(1)}, u32[]{:S(2)}, u32[]{:S(2)}) async-start(s32[128,1,1]{2,1,0:T(1,128)} %copy.37), calls=%async_computation | async-start | bytes 131072 | tf_op jit(solution)/shard_map/all_to_all | solution.py:159
  43.9 543.9 %copy-start = (bf16[1024,1024]{1,0:T(8,128)(2,1)S(1)}, bf16[1024,1024]{1,0:T(8,128)(2,1)}, u32[]{:S(2)}) copy-start(bf16[1024,1024]{1,0:T(8,128)(2,1)} %nk_ref.1) | copy-start | bytes 6291460
  43.9 543.9 %all-to-all-start.1 = ((bf16[128,1024,128]{2,1,0:T(8,128)(2,1)}), bf16[128,1024,128]{2,1,0:T(8,128)(2,1)}, u32[]{:S(2)}, u32[]{:S(2)}) async-start(bf16[128,1024,128]{2,1,0:T(8,128)(2,1)} %gather_fusion), calls=%async_computation.1 | async-start | bytes 67108864 | tf_op jit(solution)/shard_map/all_to_all | solution.py:168
  587.8 1.6 copy-start.1

commit v2 on v1

v2 whole, which is shorter than its diff:
```python
import functools
import jax
import jax.numpy as jnp
from jax import lax
from jax.experimental import pallas as pl
from jax.experimental.pallas import tpu as pltpu
from jax.sharding import PartitionSpec as P

BLOCK, HD, GROUP, TOPK = 512, 128, 4, 4
SHIFT = 1024


def segments(start, rows):
    out = []
    if start < BLOCK:
        n = min(rows, BLOCK - start)
        out.append((0, n, 0, start))
        if rows > n:
            out.append((n, rows - n, 1, 0))
    else:
        out.append((0, rows, 1, start - BLOCK))
    return out


def pick(which, refs, go):
    if len(refs) == 1:
        go(refs[0])
        return
    half = len(refs) // 2

    @pl.when(which < half)
    def _():
        pick(which, refs[:half], go)

    @pl.when(which >= half)
    def _():
        pick(which - half, refs[half:], go)


def attend_kernel(pieces, counts, spans, table, q_ref, nk_ref, nv_ref, *refs):
    total = sum(counts)
    sources = refs[:total]
    out_ref, k_buf, v_buf, nv_buf, sems = refs[-5:]
    heads, first, many = spans
    step = pl.program_id(0)
    steps = pl.num_programs(0)
    scale = HD ** -0.5 * 1.4426950408889634

    def fetch(g, slot):
        def one(j, _):
            base = 0
            for p, (start, rows) in enumerate(pieces):
                where = table[p * 8 + 4, (g // many * heads + first + lax.rem(g, many)) * TOPK + j]
                which = where // SHIFT
                row = where - which * SHIFT

                def go(ref, start=start, rows=rows, row=row):
                    for s0, length, kind, d0 in segments(start, rows):
                        if kind == 0:
                            dst = k_buf.at[slot, j, pl.ds(d0, length), :]
                        else:
                            dst = v_buf.at[slot, j, pl.ds(d0, length), pl.ds(0, HD)]
                        pltpu.make_async_copy(
                            ref.at[row, pl.ds(s0, length), :], dst, sems.at[slot]
                        ).start()

                pick(which, sources[base : base + counts[p]], go)
                base += counts[p]
            return 0

        lax.fori_loop(0, TOPK, one, 0)

    slot = lax.rem(step, 2)

    @pl.when(step == 0)
    def _():
        v_buf[:, :, :, HD:] = jnp.ones((2, TOPK, BLOCK, HD), jnp.bfloat16)
        nv_buf[:, HD:] = jnp.ones((BLOCK, HD), jnp.bfloat16)
        fetch(0, 0)

    @pl.when(step + 1 < steps)
    def _():
        fetch(step + 1, 1 - slot)

    nv_buf[:, :HD] = nv_ref[...]
    pltpu.make_async_copy(k_buf.at[slot], k_buf.at[slot], sems.at[slot]).wait()
    pltpu.make_async_copy(
        k_buf.at[slot], v_buf.at[slot, :, :, pl.ds(0, HD)], sems.at[slot]
    ).wait()

    half = 256
    dims = (((1,), (1,)), ((), ()))
    tiles = [(a, part) for a in range(GROUP) for part in range(BLOCK // half)]

    def score(n):
        a, part = tiles[n]
        keys = half * (part + 1)
        q = q_ref[pl.ds(part * half, half), pl.ds(a * HD, HD)]
        near = lax.dot_general(q, nk_ref[:keys, :], dims, preferred_element_type=jnp.float32)
        seen = lax.broadcasted_iota(jnp.int32, (half, keys), 1) <= (
            lax.broadcasted_iota(jnp.int32, (half, keys), 0) + part * half
        )
        out = [jnp.where(seen, near, -jnp.inf)]
        for j in range(TOPK):
            out.append(lax.dot_general(q, k_buf[slot, j], dims, preferred_element_type=jnp.float32))
        return out

    def finish(n, scores):
        a, part = tiles[n]
        keys = half * (part + 1)
        wide = None
        for x in scores:
            for m in range(x.shape[1] // HD):
                y = x[:, m * HD : (m + 1) * HD]
                wide = y if wide is None else jnp.maximum(wide, y)
        top = jnp.max(wide, axis=1, keepdims=True)
        top = top * scale
        values = [nv_buf[:keys, :]] + [v_buf[slot, j] for j in range(TOPK)]
        acc = None
        for x, v in zip(scores, values):
            w = jnp.exp2(x * scale - top).astype(jnp.bfloat16)
            y = jnp.dot(w, v, preferred_element_type=jnp.float32)
            acc = y if acc is None else acc + y
        out_ref[pl.ds(part * half, half), pl.ds(a * HD, HD)] = (
            acc[:, :HD] / acc[:, HD:]
        ).astype(jnp.bfloat16)

    held = score(0)
    for n in range(len(tiles)):
        later = score(n + 1) if n + 1 < len(tiles) else None
        finish(n, held)
        held = later


def attend(queries, span_keys, span_values, table, pieces, groups, first, many, before=None):
    tokens, width = queries.shape
    heads = span_keys.shape[1] // HD
    blocks = tokens // BLOCK
    counts = [len(g) for g in groups]
    flat = [s for g in groups for s in g]
    steps = blocks * many
    place = lambda g, t: (g // many, first + lax.rem(g, many))
    pairs = 2 * tokens * many * GROUP * BLOCK * (TOPK + 1)
    extra = [] if before is None else [before]
    return pl.pallas_call(
        functools.partial(attend_kernel, pieces, counts, (heads, first, many)),
        out_shape=jax.ShapeDtypeStruct((tokens, width), jnp.bfloat16),
        grid_spec=pltpu.PrefetchScalarGridSpec(
            num_scalar_prefetch=1,
            grid=(steps,),
            in_specs=[
                pl.BlockSpec((BLOCK, GROUP * HD), place),
                pl.BlockSpec((BLOCK, HD), place),
                pl.BlockSpec((BLOCK, HD), place),
            ]
            + [pl.BlockSpec(memory_space=pltpu.HBM)] * (len(flat) + len(extra)),
            out_specs=pl.BlockSpec((BLOCK, GROUP * HD), place),
            scratch_shapes=[
                pltpu.VMEM((2, TOPK, BLOCK, HD), jnp.bfloat16),
                pltpu.VMEM((2, TOPK, BLOCK, 2 * HD), jnp.bfloat16),
                pltpu.VMEM((BLOCK, 2 * HD), jnp.bfloat16),
                pltpu.SemaphoreType.DMA((2,)),
            ],
        ),
        input_output_aliases={} if before is None else {4 + len(flat): 0},
        compiler_params=pltpu.CompilerParams(
            dimension_semantics=("arbitrary",), vmem_limit_bytes=40 * 1024 * 1024
        ),
        cost_estimate=pl.CostEstimate(
            flops=4 * HD * pairs,
            transcendentals=pairs,
            bytes_accessed=6 * 1024 * 1024 * many,
        ),
        name="attend",
    )(table, queries, span_keys, span_values, *flat, *extra)


N = 128
STRIDE = (32, 8, 2)
ROWS = (352, 336, 336)
ITEMS = 16


def items_kernel(k_ref, v_ref, *outs):
    for n in range(4):
        lanes = pl.ds(n * HD, HD)
        start = 0
        for out, rows in zip(outs, ROWS):
            for s0, length, kind, d0 in segments(start, rows):
                ref = k_ref if kind == 0 else v_ref
                out[n, pl.ds(s0, length), :] = ref[0, 0, pl.ds(d0, length), lanes]
            start += rows


def cut_items(past_keys, past_values):
    spec = pl.BlockSpec((1, 1, BLOCK, 4 * HD), lambda p, n: (p, 0, 0, n))
    return pl.pallas_call(
        items_kernel,
        grid=(2, 2),
        in_specs=[spec, spec],
        out_specs=[pl.BlockSpec((4, r, HD), lambda p, n: (p * 2 + n, 0, 0)) for r in ROWS],
        out_shape=[jax.ShapeDtypeStruct((ITEMS, r, HD), jnp.bfloat16) for r in ROWS],
        name="cut_items",
    )(past_keys, past_values)


def plan_kernel(cut, caps2, caps3, place, w_ref, req_ref, out_ref):
    f32, bf16, i32 = jnp.float32, jnp.bfloat16, jnp.int32
    c = place[3]
    s = 1 - 2 * c
    wanted = w_ref[...].astype(f32).astype(bf16)
    lane = lax.broadcasted_iota(i32, (1, N), 1)
    sub = lax.broadcasted_iota(i32, (N, N), 0)
    lanes = lax.broadcasted_iota(i32, (N, N), 1)
    sub8 = lax.broadcasted_iota(i32, (8, N), 0)
    lane8 = lax.broadcasted_iota(i32, (8, N), 1)
    below = jnp.where(sub < lanes, 1.0, 0.0).astype(bf16)

    def mm(a, b):
        return jnp.dot(a.astype(bf16), b.astype(bf16), preferred_element_type=f32)

    def hot(row):
        return jnp.where(sub == row, 1.0, 0.0).astype(bf16)

    def stack(rows):
        out = jnp.zeros((8, N), rows[0].dtype)
        for n, row in enumerate(rows):
            out = jnp.where(sub8 == n, row, out)
        return out

    def spread(rows, chosen):
        codes = stack([r.astype(f32) for r in rows]).astype(bf16)
        out = lax.dot_general(
            codes,
            jnp.where(chosen, 1.0, 0.0).astype(bf16),
            (((1,), (1,)), ((), ())),
            preferred_element_type=f32,
        ).astype(i32)
        return out[0:1] * SHIFT + out[1:2]

    def ranked(needs, early):
        low = needs * early
        high = needs - low
        after = jnp.sum(low, axis=1, keepdims=True)
        return jnp.where(early > 0.5, mm(low, below), mm(high, below) + after)

    def seat(rank, turn, caps, base_a, base_b):
        na, nb = caps
        late = jnp.where(rank >= na, 1, 0)
        here = rank - late * na
        limit = jnp.where(late == 1, nb // 2, na // 2)
        half = jnp.where(here >= limit, 1, 0)
        buf = jnp.where(turn == 3, 0, jnp.where(turn == 1, 1, jnp.where(half == c, 2, 3)))
        pos = jnp.where(turn == 2, here - half * limit, here)
        return buf + jnp.where(late == 1, base_b, base_a), pos

    def seats(caps, late, rank_near, need_near, rank_far, need_far):
        skip = caps[0] if late else 0
        cap = caps[1] if late else caps[0]
        near_side = jnp.where((rank_near == sub + skip) & (sub < cap), need_near, 0.0) > 0.5
        far_side = (
            jnp.where(
                (rank_far == sub - cap + c * (cap // 2) + skip) & (sub >= cap) & (sub < cap + cap // 2),
                need_far,
                0.0,
            )
            > 0.5
        )
        return near_side, far_side

    for t in range(3):
        a1, a2, a3 = t, (t + 1) % 3, (t + 2) % 3
        s1, s2, s3 = STRIDE[a1], STRIDE[a2], STRIDE[a3]
        at1, at2, at3 = place[a1], place[a2], place[a3]

        o1, oc, item = lane >> 5, (lane >> 4) & 1, lane & 15
        rows = []
        for v in (at2, (at2 + s) & 3, (at2 + 2) & 3):
            who = at1 * s1 + v * s2 + (sub8 >> 1) * s3 + (sub8 & 1)
            rows.append(mm(jnp.where(lane8 == who, 1.0, 0.0), wanted))
        needs = []
        for q in range(4):
            got = mm(rows[0], hot(o1 * s1 + q * s2 + at3 * s3 + oc))
            needs.append(jnp.max(jnp.where(got.astype(i32) == item + 1, 1.0, 0.0), axis=0, keepdims=True))
        mine = hot(o1 * s1 + at2 * s2 + at3 * s3 + oc)
        for n in (1, 2):
            got = mm(rows[n], mine)
            needs.append(jnp.max(jnp.where(got.astype(i32) == item + 1, 1.0, 0.0), axis=0, keepdims=True))
        needs2 = stack(needs)
        rank2 = ranked(needs2, jnp.where((lane8 & 7) < cut, 1.0, 0.0))
        ranks2 = rank2.astype(i32)

        def first(b1, bc, bi):
            r1 = ((b1 - at1) * s) & 3
            same = bc == c
            buf = jnp.where(r1 == 0, jnp.where(same, 0, 1), jnp.where(r1 == 3, jnp.where(same, 2, 3), jnp.where(r1 == 1, jnp.where(same, 5, 4), jnp.where(same, 6, 7))))
            return buf, bi

        def second(b1, b2, bc, bi):
            buf, pos = first(b1, bc, bi)
            found = mm(rank2, hot((b1 * 2 + bc) * ITEMS + bi)).astype(i32)
            rank = jnp.zeros((1, N), i32)
            for q in range(4):
                rank = jnp.where(b2 == q, found[q : q + 1], rank)
            r2 = ((b2 - at2) * s) & 3
            far_buf, far_pos = seat(rank, r2, caps2, 8, 12)
            return jnp.where(r2 == 0, buf, far_buf), jnp.where(r2 == 0, pos, far_pos)

        packed = []
        for late in (0, 1):
            near_side, far_side = seats(
                caps2, late, ranks2[4:5], needs2[4:5], ranks2[5:6], needs2[5:6]
            )
            packed.append(spread(first(o1, oc, item), near_side | far_side))

        rc, o1, o2, oc = lane >> 5, (lane >> 3) & 3, (lane >> 1) & 3, lane & 1
        turn = sub8 >> 1
        v = jnp.where(turn == 0, at3, jnp.where(turn == 1, (at3 + s) & 3, (at3 + 2) & 3))
        who = jnp.where(sub8 < 6, at1 * s1 + at2 * s2 + v * s3 + (sub8 & 1), -1)
        asked = mm(jnp.where(lane8 == who, 1.0, 0.0), wanted)
        values = []
        for q in range(4):
            got = mm(asked, hot(o1 * s1 + o2 * s2 + q * s3 + oc))
            values.append(jnp.where(rc == 0, got[0:1], got[1:2]))
        got = mm(asked, hot(o1 * s1 + o2 * s2 + at3 * s3 + oc))
        values.append(jnp.where(rc == 0, got[2:3], got[3:4]))
        values.append(jnp.where(rc == 0, got[4:5], got[5:6]))
        values = stack(values)
        needs3 = jnp.where((values > 0.5) & (lane8 < 64), 1.0, 0.0)
        which = jnp.maximum(values.astype(i32) - 1, 0)
        rank3 = ranked(needs3, jnp.where((which & 7) < cut, 1.0, 0.0))
        ranks3 = rank3.astype(i32)
        for late in (0, 1):
            near_side, far_side = seats(
                caps3, late, ranks3[4:5], needs3[4:5], ranks3[5:6], needs3[5:6]
            )
            packed.append(
                spread(second(o1, o2, oc, which[4:5]), near_side)
                + spread(second(o1, o2, oc, which[5:6]), far_side)
            )

        owner, item = req_ref[0:1, :], req_ref[1:2, :]
        digit = lambda stride: (owner >> (stride.bit_length() - 1)) & 3
        o1, o2, o3, oc = digit(s1), digit(s2), digit(s3), owner & 1
        buf, pos = second(o1, o2, oc, item)
        found = mm(rank3, hot(c * 32 + o1 * 8 + o2 * 2 + oc)).astype(i32)
        rank = jnp.zeros((1, N), i32)
        for q in range(4):
            rank = jnp.where(o3 == q, found[q : q + 1], rank)
        r3 = ((o3 - at3) * s) & 3
        far_buf, far_pos = seat(rank, r3, caps3, jnp.where((item & 7) < cut, 12, 16), 20)
        final = jnp.where(r3 == 0, buf, far_buf) * SHIFT + jnp.where(r3 == 0, pos, far_pos)
        out_ref[pl.ds(t * 8, 8), :] = stack([*packed, final])


def check_kernel(cut, w_ref, out_ref):
    f32, bf16, i32 = jnp.float32, jnp.bfloat16, jnp.int32
    wanted = w_ref[...]
    digit = lambda x, stride: (x >> (stride.bit_length() - 1)) & 3
    row48 = lax.broadcasted_iota(i32, (48, N), 0)
    lane48 = lax.broadcasted_iota(i32, (48, N), 1)
    sub = lax.broadcasted_iota(i32, (N, N), 0)
    lanes = lax.broadcasted_iota(i32, (N, N), 1)

    def mm(a, b):
        return jnp.dot(a.astype(bf16), b.astype(bf16), preferred_element_type=f32)

    groups = jnp.zeros((48, N), f32)
    for t in range(3):
        s1, s2 = STRIDE[t], STRIDE[(t + 1) % 3]
        hit = row48 == t * 16 + digit(lane48, s1) * 4 + digit(lane48, s2)
        groups = jnp.where(hit, 1.0, groups)
    sums = [jnp.zeros((48, N), f32), jnp.zeros((48, N), f32)]
    for n in range(ITEMS):
        any_wants = mm(groups, jnp.where(wanted == n + 1, 1.0, 0.0)) > 0.5
        late = 0 if (n & 7) < cut else 1
        sums[late] += jnp.where(any_wants, 1.0, 0.0)
    early2, all2 = jnp.zeros((48, N), f32), jnp.zeros((48, N), f32)
    for t in range(3):
        s2, s3 = STRIDE[(t + 1) % 3], STRIDE[(t + 2) % 3]
        owners = jnp.where(lanes == digit(sub, s2) * 4 + digit(sub, s3), 1.0, 0.0)
        keep = (row48 >> 4 == t) & ((row48 & 3) != (lane48 >> 2)) & (lane48 < 16)
        early = mm(sums[0], owners)
        early2 = jnp.where(keep, early, early2)
        all2 = jnp.where(keep, early + mm(sums[1], owners), all2)
    chip = lax.broadcasted_iota(i32, (64, N), 0)
    lane64 = lax.broadcasted_iota(i32, (64, N), 1)
    pairs = jnp.where(lane64 >> 1 == chip, 1.0, 0.0)
    low = jnp.where((wanted > 0) & (((wanted - 1) & 7) < cut), 1.0, 0.0)
    every = jnp.where(wanted > 0, 1.0, 0.0)
    owners = jnp.zeros((N, N), f32)
    keep = lane64 < 12
    for t in range(3):
        s3 = STRIDE[(t + 2) % 3]
        owners = jnp.where(lanes == t * 4 + digit(sub, s3), 1.0, owners)
        keep = keep & (lane64 != t * 4 + digit(chip * 2, s3))
    early3 = jnp.where(keep, mm(mm(pairs, low), owners), 0.0)
    all3 = jnp.where(keep, mm(mm(pairs, every), owners), 0.0)
    out = jnp.zeros((8, N), f32)
    sub8 = lax.broadcasted_iota(i32, (8, N), 0)
    for n, x in enumerate((early2, all2, early3, all3)):
        top = jnp.max(jnp.max(x, axis=1, keepdims=True), axis=0, keepdims=True)
        out = jnp.where(sub8 == n, top, out)
    out_ref[...] = out.astype(i32)


def longest(cut, wanted):
    return pl.pallas_call(
        functools.partial(check_kernel, cut),
        out_shape=jax.ShapeDtypeStruct((8, N), jnp.int32),
        in_specs=[pl.BlockSpec(memory_space=pltpu.VMEM)],
        out_specs=pl.BlockSpec(memory_space=pltpu.VMEM),
        name="longest",
    )(wanted)


def make_plan(cut, caps2, caps3, place, wanted, requests):
    return pl.pallas_call(
        functools.partial(plan_kernel, cut, caps2, caps3),
        out_shape=jax.ShapeDtypeStruct((24, N), jnp.int32),
        grid_spec=pltpu.PrefetchScalarGridSpec(
            num_scalar_prefetch=1,
            grid=(1,),
            in_specs=[
                pl.BlockSpec((N, N), lambda i, t: (0, 0)),
                pl.BlockSpec((8, N), lambda i, t: (0, 0)),
            ],
            out_specs=pl.BlockSpec((24, N), lambda i, t: (0, 0)),
        ),
        name="plan",
    )(place, wanted, requests)


def pack_kernel(row, first, count, n_sources, table, *refs):
    sources, out, sem = refs[:n_sources], refs[n_sources], refs[n_sources + 1]

    def one(k, _):
        where = table[row, first + k]
        which = where // SHIFT
        pos = where - which * SHIFT
        pick(which, sources, lambda ref: pltpu.make_async_copy(ref.at[pos], out.at[k], sem).start())
        return 0

    lax.fori_loop(0, count, one, 0)
    pltpu.make_async_copy(out, out, sem).wait()


def pack(table, row, first, count, sources):
    rows = sources[0].shape[1]
    return pl.pallas_call(
        functools.partial(pack_kernel, row, first, count, len(sources)),
        out_shape=jax.ShapeDtypeStruct((count, rows, HD), jnp.bfloat16),
        in_specs=[pl.BlockSpec(memory_space=pltpu.SMEM)]
        + [pl.BlockSpec(memory_space=pltpu.HBM)] * len(sources),
        out_specs=pl.BlockSpec(memory_space=pltpu.VMEM),
        scratch_shapes=[pltpu.SemaphoreType.DMA],
        compiler_params=pltpu.CompilerParams(vmem_limit_bytes=24 * 1024 * 1024),
        name="pack",
    )(table, *sources)


def ring_pairs(axis):
    pairs = []
    for i in range(N):
        at = (i // STRIDE[axis]) % 4
        to = (at + (1 if i % 2 == 0 else 3)) % 4
        pairs.append((i, i + (to - at) * STRIDE[axis]))
    return pairs


def onward(x, axis):
    return lax.ppermute(x, "seq", ring_pairs(axis))


def swap(x):
    return lax.ppermute(x, "seq", [(i, i ^ 1) for i in range(N)])


def hop(pools, table, row, axis_of, cap):
    half = cap // 2
    packed = [pack(table, t * 8 + row, cap, half, pools[t]) for t in range(3)]
    table, packed = lax.optimization_barrier((table, packed))
    through = [onward(packed[t], axis_of(t)) for t in range(3)]
    direct = [onward(pack(table, t * 8 + row, 0, cap, pools[t]), axis_of(t)) for t in range(3)]
    passed = [onward(through[t], axis_of(t)) for t in range(3)]
    return [[direct[t], swap(direct[t]), passed[t], swap(passed[t])] for t in range(3)]


def join(*lists):
    return [sum((x[t] for x in lists), []) for t in range(3)]


def route(cut, caps2, caps3, splits, queries, span_keys, span_values, pools, place, wanted, requests, table):
    if caps2 != FAST[1]:
        table = make_plan(cut, caps2, caps3, place, wanted, requests)
    side = lambda t: (t + 1) % 3
    last = lambda t: (t + 2) % 3
    starts = (0, ROWS[0], ROWS[0] + ROWS[1])
    pieces = list(zip(starts, ROWS))
    two_a = hop(pools, table, 0, side, caps2[0])
    three_a = hop(join(pools, two_a), table, 2, last, caps3[0])
    groups = [join(pools, two_a, three_a)]
    if caps2[1]:
        two_b = hop(pools, table, 1, side, caps2[1])
        three_b = hop(join(pools, two_a, two_b), table, 3, last, caps3[1])
        groups.append(join(pools, two_a, two_b, three_a, three_b))
    out = None
    for ranges, found in zip(splits, groups):
        for first, many in ranges:
            out = attend(queries, span_keys, span_values, table, pieces, found, first, many, out)
    return out


FAST = (8, (44, 0), (48, 0), (((0, 8),),))
SAFE = (8, (64, 0), (64, 0), (((0, 8),),))


def shards(queries, span_keys, span_values, past_keys, past_values, selected):
    heads = selected.shape[1]
    me = lax.axis_index("seq")
    place = jnp.stack([me // 32, me // 8 % 4, me // 2 % 4, me % 2]).astype(jnp.int32)
    chosen = selected.reshape(-1)
    owners = chosen % N
    item = chosen // N * heads + lax.broadcasted_iota(jnp.int32, selected.shape, 1).reshape(-1)
    match = owners[None, :] == jnp.arange(N, dtype=jnp.int32)[:, None]
    outgoing = jnp.sum(jnp.where(match, item[None, :] + 1, 0), axis=1)
    copies = jnp.broadcast_to(outgoing, (N, 1, N))
    wanted = lax.all_to_all(copies, "seq", split_axis=0, concat_axis=0, tiled=True).reshape(N, N)
    requests = jnp.pad(jnp.stack([owners, item]), ((0, 6), (0, N - owners.shape[0])))

    own = cut_items(past_keys, past_values)
    ahead = [onward(own[t], t) for t in range(3)]
    raw = [swap(past_keys), swap(past_values)]
    raw, wanted = lax.optimization_barrier((raw, wanted))
    mate = cut_items(*raw)
    ahead_mate = [onward(mate[t], t) for t in range(3)]
    table = make_plan(*FAST[:3], place, wanted, requests)
    most = longest(FAST[0], wanted)[:4, 0]
    fits = jnp.all(most <= jnp.array([FAST[1][0], sum(FAST[1]), FAST[2][0], sum(FAST[2])]))
    ahead, table, fits = lax.optimization_barrier((ahead, table, fits))
    twice = [onward(ahead[t], t) for t in range(3)]
    pools = [
        [own[t], mate[t], ahead[t], ahead_mate[t], swap(ahead[t]), swap(ahead_mate[t]), twice[t], swap(twice[t])]
        for t in range(3)
    ]
    args = (queries, span_keys, span_values, pools, place, wanted, requests, table)
    return lax.cond(
        fits, functools.partial(route, *FAST), functools.partial(route, *SAFE), *args
    )


def solution(mesh):
    return jax.shard_map(
        shards,
        mesh=mesh,
        in_specs=(
            P("seq", None),
            P("seq", None),
            P("seq", None),
            P(None, "seq", None, None),
            P(None, "seq", None, None),
            P("seq", None, None),
        ),
        out_specs=P("seq", None),
        check_vma=False,
    )
```

time: 713 us -> 521 us (0.73)
  the two profiles are of different devices: /device:TPU:122 before, /device:TPU:1 now
where the time goes in v2:
time: 521 us; the launch traced here: 512 us
  waiting for transfers between devices  221 us (42%)
  Pallas kernels  196 us (38%)
  starting transfers between devices  71.8 us (14%)
  local copies, waits for them, and re-layouts  11.3 us (2%)
  loops' own time  9.03 us (2%)
    ppermute x27, waiting for transfers between devices, onward(): return lax.ppermute(x, 'seq', ring_pairs(axis))  192 us
    pallas_call x1, Pallas kernels, attend(): pl.pallas_call(functools.partial(attend_kernel, pieces, counts, (heads, f...  114 us
    pallas_call x12, Pallas kernels, pack(): pl.pallas_call(functools.partial(pack_kernel, row, first, count, len(sour...  67.6 us
    ppermute x23, starting transfers between devices, swap(): return lax.ppermute(x, 'seq', [(i, i ^ 1) for i in range(N)])  39.9 us
    ppermute x27, starting transfers between devices, onward(): return lax.ppermute(x, 'seq', ring_pairs(axis))  26.5 us
    ppermute x23, waiting for transfers between devices, swap(): return lax.ppermute(x, 'seq', [(i, i ^ 1) for i in range(N)])  17.5 us
    all_to_all x1, waiting for transfers between devices, shards(): lax.all_to_all(copies, 'seq', split_axis=0, concat_axis=0, tiled=True)  11.9 us
  transfers between devices with their start and end apart: 51, of which 21 were waited for; matrix products, arithmetic and copies ran while one was open for 0% of the time, Pallas kernels for 13%

profile of v2, /device:TPU:1, one launch (start us, length us, event | category | flops | bytes accessed | tf_op | source)
XLA Modules:
  0.0 512.2 jit_solution(7602704812610528742)
XLA Ops:
  1.4 4.5 cut_items.2
  6.0 2.6 collective-permute-start.60
  8.6 3.8 collective-permute-start.61
  12.4 2.7 collective-permute-start.62
  16.2 5.4 %all-to-all-start = ((s32[128,1,128]{2,1,0:T(1,128)}), s32[128,1,128]{2,1,0:T(1,128)S(1)}, u32[]{:S(2)}, u32[]{:S(2)}) async-start(s32[128,1,128]{2,1,0:T(1,128)} %broadcast_in_dim.20), calls=%async_computation | async-start | bytes 131072 | tf_op jit(solution)/shard_map/all_to_all | solution.py:528
  22.0 11.9 %all-to-all-done = s32[128,1,128]{2,1,0:T(1,128)S(1)} async-done(((s32[128,1,128]{2,1,0:T(1,128)}), s32[128,1,128]{2,1,0:T(1,128)S(1)}, u32[]{:S(2)}, u32[]{:S(2)}) %all-to-all-start) | async-done | bytes 65568 | tf_op jit(solution)/shard_map/all_to_all | solution.py:528
  35.1 4.9 cut_items.3
  40.8 2.1 collective-permute-start.75
  42.9 3.4 plan.3
  49.2 8.6 %collective-permute-done.70 = bf16[16,336,128]{2,1,0:T(8,128)(2,1)} collective-permute-done((bf16[16,336,128]{2,1,0:T(8,128)(2,1)}, bf16[16,336,128]{2,1,0:T(8,128)(2,1)}, u32[]{:S(2)}, u32[]{:S(2)}) %collective-permute-start.70) | collective-permute-done | bytes 1376288 | tf_op jit(solution)/shard_map/ppermute | solution.py:472
  60.5 12.0 %collective-permute-done.73 = bf16[16,336,128]{2,1,0:T(8,128)(2,1)} collective-permute-done((bf16[16,336,128]{2,1,0:T(8,128)(2,1)}, bf16[16,336,128]{2,1,0:T(8,128)(2,1)}, u32[]{:S(2)}, u32[]{:S(2)}) %collective-permute-start.73) | collective-permute-done | bytes 1376288 | tf_op jit(solution)/shard_map/ppermute | solution.py:472
  72.5 2.7 collective-permute-start.66
  76.3 4.8 collective-permute-start.67
  81.1 10.6 %collective-permute-done.68 = bf16[16,352,128]{2,1,0:T(8,128)(2,1)} collective-permute-done((bf16[16,352,128]{2,1,0:T(8,128)(2,1)S(1)}, bf16[16,352,128]{2,1,0:T(8,128)(2,1)}, u32[]{:S(2)}, u32[]{:S(2)}) %collective-permute-start.68) | collective-permute-done | bytes 1441824 | tf_op jit(solution)/shard_map/ppermute | solution.py:472
  91.7 4.8 collective-permute-start.69
  105.6 405.2 %conditional.1 = (bf16[1024,4096]{1,0:T(8,128)(2,1)}) conditional(s32[]{:T(128)} %convert_element_type.3, (s32[4]{0:T(128)S(1)}, s32[128,128]{1,0:T(8,128)S(1)}, s32[8,128]{1,0:T(8,128)S(1)}, bf16[16,352,128]{2,1,0:T(8,128)(2,1)S(1)}, bf16[16,352,128]{2,1,0:T(8,128)(2,1)}, /*index=5*/bf16[16,352,128]{2,1,0:T(8,128)(2,1)S(1)}, ...), branch_computations={%region_2.3_spmd, %region_3.4_spmd} | conditional | flops 85899345920 | bytes 933594496 | solution.py:547
  113.9 3.6 pack.37
  117.7 3.8 pack.38
  121.5 3.5 pack.36
  125.9 5.6 %pack.39 = bf16[44,352,128]{2,1,0:T(8,128)(2,1)S(1)} custom-call(s32[24,128]{1,0:T(8,128)S(1)} %get-tuple-element.194.table, bf16[16,352,128]{2,1,0:T(8,128)(2,1)S(1)} %get-tuple-element.166.refs_0_, bf16[16,352,128]{2,1,0:T(8,128)(2,1)S(1)} %copy-done.42, bf16[16,352,128]{2,1,0:T(8,128)(2,1)S(1)} %get-tuple-element.168.refs_2_, ...), custom_call_target="tpu_custom_call" | custom-call | tf_op jit(solution)/shard_map/cond/branch_1_fun/pack/pallas_call | solution.py:450
  133.4 5.9 %pack.41 = bf16[44,336,128]{2,1,0:T(8,128)(2,1)S(1)} custom-call(s32[24,128]{1,0:T(8,128)S(1)} %get-tuple-element.194.table, bf16[16,336,128]{2,1,0:T(8,128)(2,1)S(1)} %copy-done.47, bf16[16,336,128]{2,1,0:T(8,128)(2,1)S(1)} %copy-done.52, bf16[16,336,128]{2,1,0:T(8,128)(2,1)} %get-tuple-element.176.refs_2_.refs_18_, ...), custom_call_target="tpu_custom_call" | custom-call | tf_op jit(solution)/shard_map/cond/branch_1_fun/pack/pallas_call | solution.py:450
  139.6 5.6 %pack.43 = bf16[44,336,128]{2,1,0:T(8,128)(2,1)S(1)} custom-call(s32[24,128]{1,0:T(8,128)S(1)} %get-tuple-element.194.table, bf16[16,336,128]{2,1,0:T(8,128)(2,1)S(1)} %copy-done.49, bf16[16,336,128]{2,1,0:T(8,128)(2,1)S(1)} %copy-done.55, bf16[16,336,128]{2,1,0:T(8,128)(2,1)} %get-tuple-element.184.refs_2_.refs_34_, ...), custom_call_target="tpu_custom_call" | custom-call | tf_op jit(solution)/shard_map/cond/branch_1_fun/pack/pallas_call | solution.py:450
  145.2 3.0 collective-permute-done.37
  149.0 7.2 %collective-permute-done.42 = bf16[22,336,128]{2,1,0:T(8,128)(2,1)S(1)} collective-permute-done((bf16[22,336,128]{2,1,0:T(8,128)(2,1)S(1)}, bf16[22,336,128]{2,1,0:T(8,128)(2,1)S(1)}, u32[]{:S(2)}, u32[]{:S(2)}) %collective-permute-start.42) | collective-permute-done | bytes 1892384 | tf_op jit(solution)/shard_map/cond/branch_1_fun/ppermute | solution.py:472
  156.6 41.5 %collective-permute-done.32 = bf16[22,352,128]{2,1,0:T(8,128)(2,1)S(1)} collective-permute-done((bf16[22,352,128]{2,1,0:T(8,128)(2,1)S(1)}, bf16[22,352,128]{2,1,0:T(8,128)(2,1)S(1)}, u32[]{:S(2)}, u32[]{:S(2)}) %collective-permute-start.32) | collective-permute-done | bytes 1982496 | tf_op jit(solution)/shard_map/cond/branch_1_fun/ppermute | solution.py:472
  198.9 10.0 %collective-permute-done.38.refs_10_.refs_26_ = bf16[22,336,128]{2,1,0:T(8,128)(2,1)S(1)} collective-permute-done((bf16[22,336,128]{2,1,0:T(8,128)(2,1)}, bf16[22,336,128]{2,1,0:T(8,128)(2,1)S(1)}, u32[]{:S(2)}, u32[]{:S(2)}) %collective-permute-start.38) | collective-permute-done | bytes 1892384 | tf_op jit(solution)/shard_map/cond/branch_1_fun/ppermute | solution.py:472
  209.1 2.3 collective-permute-start.31
  211.6 9.4 %collective-permute-done.43.refs_10_.refs_42_ = bf16[22,336,128]{2,1,0:T(8,128)(2,1)S(1)} collective-permute-done((bf16[22,336,128]{2,1,0:T(8,128)(2,1)S(1)}, bf16[22,336,128]{2,1,0:T(8,128)(2,1)S(1)}, u32[]{:S(2)}, u32[]{:S(2)}) %collective-permute-start.43) | collective-permute-done | bytes 1892384 | tf_op jit(solution)/shard_map/cond/branch_1_fun/ppermute | solution.py:472
  221.0 4.5 collective-permute-start.39
  225.6 7.3 %collective-permute-done.33.refs_10_ = bf16[22,352,128]{2,1,0:T(8,128)(2,1)S(1)} collective-permute-done((bf16[22,352,128]{2,1,0:T(8,128)(2,1)S(1)}, bf16[22,352,128]{2,1,0:T(8,128)(2,1)S(1)}, u32[]{:S(2)}, u32[]{:S(2)}) %collective-permute-start.33) | collective-permute-done | bytes 1982496 | tf_op jit(solution)/shard_map/cond/branch_1_fun/ppermute | solution.py:472
  232.9 4.5 collective-permute-start.34
  237.5 5.3 %pack.42 = bf16[24,336,128]{2,1,0:T(8,128)(2,1)} custom-call(s32[24,128]{1,0:T(8,128)S(1)} %get-tuple-element.194.table, bf16[16,336,128]{2,1,0:T(8,128)(2,1)S(1)} %copy-done.47, bf16[16,336,128]{2,1,0:T(8,128)(2,1)S(1)} %copy-done.53, bf16[16,336,128]{2,1,0:T(8,128)(2,1)} %get-tuple-element.176.refs_2_.refs_18_, ...), custom_call_target="tpu_custom_call" | custom-call | tf_op jit(solution)/shard_map/cond/branch_1_fun/pack/pallas_call | solution.py:450
  243.7 5.4 %pack.44 = bf16[24,336,128]{2,1,0:T(8,128)(2,1)} custom-call(s32[24,128]{1,0:T(8,128)S(1)} %get-tuple-element.194.table, bf16[16,336,128]{2,1,0:T(8,128)(2,1)} %get-tuple-element.182.refs_0_.refs_32_, bf16[16,336,128]{2,1,0:T(8,128)(2,1)} %get-tuple-element.183.refs_1_.refs_33_, bf16[16,336,128]{2,1,0:T(8,128)(2,1)} %get-tuple-element.184.refs_2_.refs_34_, ...), custom_call_target="tpu_custom_call" | custom-call | tf_op jit(solution)/shard_map/cond/branch_1_fun/pack/pallas_call | solution.py:450
  249.2 5.9 %pack.40 = bf16[24,352,128]{2,1,0:T(8,128)(2,1)} custom-call(s32[24,128]{1,0:T(8,128)S(1)} %get-tuple-element.194.table, bf16[16,352,128]{2,1,0:T(8,128)(2,1)S(1)} %copy-done.36, bf16[16,352,128]{2,1,0:T(8,128)(2,1)} %get-tuple-element.167.refs_1_, bf16[16,352,128]{2,1,0:T(8,128)(2,1)S(1)} %copy-done.39, bf16[16,352,128]{2,1,0:T(8,128)(2,1)} %get-tuple-element.169.refs_3_, ...), custom_call_target="tpu_custom_call" | custom-call | tf_op jit(solution)/shard_map/cond/branch_1_fun/pack/pallas_call | solution.py:450
  255.2 9.3 %pack.45 = bf16[48,352,128]{2,1,0:T(8,128)(2,1)} custom-call(s32[24,128]{1,0:T(8,128)S(1)} %get-tuple-element.194.table, bf16[16,352,128]{2,1,0:T(8,128)(2,1)S(1)} %copy-done.36, bf16[16,352,128]{2,1,0:T(8,128)(2,1)} %get-tuple-element.167.refs_1_, bf16[16,352,128]{2,1,0:T(8,128)(2,1)S(1)} %copy-done.39, bf16[16,352,128]{2,1,0:T(8,128)(2,1)} %get-tuple-element.169.refs_3_, ...), custom_call_target="tpu_custom_call" | custom-call | tf_op jit(solution)/shard_map/cond/branch_1_fun/pack/pallas_call | solution.py:450
  264.9 6.9 %pack.46 = bf16[48,336,128]{2,1,0:T(8,128)(2,1)S(1)} custom-call(s32[24,128]{1,0:T(8,128)S(1)} %get-tuple-element.194.table, bf16[16,336,128]{2,1,0:T(8,128)(2,1)} %get-tuple-element.174.refs_0_.refs_16_, bf16[16,336,128]{2,1,0:T(8,128)(2,1)} %get-tuple-element.175.refs_1_.refs_17_, bf16[16,336,128]{2,1,0:T(8,128)(2,1)} %get-tuple-element.176.refs_2_.refs_18_, ...), custom_call_target="tpu_custom_call" | custom-call | tf_op jit(solution)/shard_map/cond/branch_1_fun/pack/pallas_call | solution.py:450
  271.8 2.0 collective-permute-start.50
  273.8 7.0 %pack.47 = bf16[48,336,128]{2,1,0:T(8,128)(2,1)S(1)} custom-call(s32[24,128]{1,0:T(8,128)S(1)} %get-tuple-element.194.table, bf16[16,336,128]{2,1,0:T(8,128)(2,1)S(1)} %copy-done.50, bf16[16,336,128]{2,1,0:T(8,128)(2,1)S(1)} %copy-done.56, bf16[16,336,128]{2,1,0:T(8,128)(2,1)} %get-tuple-element.184.refs_2_.refs_34_, ...), custom_call_target="tpu_custom_call" | custom-call | tf_op jit(solution)/shard_map/cond/branch_1_fun/pack/pallas_call | solution.py:450
  280.9 8.8 %collective-permute-done.57 = bf16[24,336,128]{2,1,0:T(8,128)(2,1)} collective-permute-done((bf16[24,336,128]{2,1,0:T(8,128)(2,1)}, bf16[24,336,128]{2,1,0:T(8,128)(2,1)}, u32[]{:S(2)}, u32[]{:S(2)}) %collective-permute-start.57) | collective-permute-done | bytes 2064416 | tf_op jit(solution)/shard_map/cond/branch_1_fun/ppermute | solution.py:472
  291.6 45.4 %collective-permute-done.47 = bf16[24,352,128]{2,1,0:T(8,128)(2,1)} collective-permute-done((bf16[24,352,128]{2,1,0:T(8,128)(2,1)}, bf16[24,352,128]{2,1,0:T(8,128)(2,1)}, u32[]{:S(2)}, u32[]{:S(2)}) %collective-permute-start.47) | collective-permute-done | bytes 2162720 | tf_op jit(solution)/shard_map/cond/branch_1_fun/ppermute | solution.py:472
  337.1 9.4 %collective-permute-done.53.refs_30_ = bf16[24,336,128]{2,1,0:T(8,128)(2,1)S(1)} collective-permute-done((bf16[24,336,128]{2,1,0:T(8,128)(2,1)}, bf16[24,336,128]{2,1,0:T(8,128)(2,1)S(1)}, u32[]{:S(2)}, u32[]{:S(2)}) %collective-permute-start.53) | collective-permute-done | bytes 2064416 | tf_op jit(solution)/shard_map/cond/branch_1_fun/ppermute | solution.py:472
  346.5 2.6 collective-permute-start.46
  349.2 13.0 %collective-permute-done.58.refs_46_ = bf16[24,336,128]{2,1,0:T(8,128)(2,1)S(1)} collective-permute-done((bf16[24,336,128]{2,1,0:T(8,128)(2,1)}, bf16[24,336,128]{2,1,0:T(8,128)(2,1)S(1)}, u32[]{:S(2)}, u32[]{:S(2)}) %collective-permute-start.58) | collective-permute-done | bytes 2064416 | tf_op jit(solution)/shard_map/cond/branch_1_fun/ppermute | solution.py:472
  362.1 5.0 collective-permute-start.54
  367.7 4.9 collective-permute-done.48.refs_14_
  372.6 4.7 collective-permute-start.49
  377.7 11.1 %collective-permute-done.59.refs_47_ = bf16[24,336,128]{2,1,0:T(8,128)(2,1)S(1)} collective-permute-done((bf16[24,336,128]{2,1,0:T(8,128)(2,1)S(1)}, bf16[24,336,128]{2,1,0:T(8,128)(2,1)S(1)}, u32[]{:S(2)}, u32[]{:S(2)}) %collective-permute-start.59) | collective-permute-done | bytes 2064416 | tf_op jit(solution)/shard_map/cond/branch_1_fun/ppermute | solution.py:476
  396.4 114.2 %attend.3 = bf16[1024,4096]{1,0:T(8,128)(2,1)} custom-call(s32[24,128]{1,0:T(8,128)S(1)} %get-tuple-element.194.table, bf16[1024,4096]{1,0:T(8,128)(2,1)} %get-tuple-element.163.q_ref, bf16[1024,1024]{1,0:T(8,128)(2,1)} %get-tuple-element.164.nk_ref, bf16[1024,1024]{1,0:T(8,128)(2,1)} %get-tuple-element.165.nv_ref, bf16[16,352,128]{2,1,0:T(8,128)(2,1)S(1)} %copy-done.36, ...), custom_call_target="tpu_custom_call" | custom-call | flops 85899345920 | bytes 50331648 | tf_op jit(solution)/shard_map/cond/branch_1_fun/attend/pallas_call | solution.py:145
  (185 shorter events, 37.4 us)
Async XLA Ops:
  0.0 33.9 %collective-permute-start.63 = (bf16[2,1,512,1024]{3,2,1,0:T(8,128)(2,1)}, bf16[2,1,512,1024]{3,2,1,0:T(8,128)(2,1)}, u32[]{:S(2)}, u32[]{:S(2)}) collective-permute-start(bf16[2,1,512,1024]{3,2,1,0:T(8,128)(2,1)} %k_ref.1), channel_id=1, source_target_pairs={{0,1},{1,0},{2,3},{3,2},{4,5},{5,4},{6,7},{7,6},{8,9},{9,8},{10,11... | collective-permute-start | bytes 6291464 | tf_op jit(solution)/shard_map/ppermute | solution.py:476
  1.4 32.5 %collective-permute-start.64 = (bf16[2,1,512,1024]{3,2,1,0:T(8,128)(2,1)}, bf16[2,1,512,1024]{3,2,1,0:T(8,128)(2,1)}, u32[]{:S(2)}, u32[]{:S(2)}) collective-permute-start(bf16[2,1,512,1024]{3,2,1,0:T(8,128)(2,1)} %v_ref.1), channel_id=1, source_target_pairs={{0,1},{1,0},{2,3},{3,2},{4,5},{5,4},{6,7},{7,6},{8,9},{9,8},{10,11... | collective-permute-start | bytes 6291464 | tf_op jit(solution)/shard_map/ppermute | solution.py:476
  6.0 41.0 %collective-permute-start.60 = (bf16[16,352,128]{2,1,0:T(8,128)(2,1)S(1)}, bf16[16,352,128]{2,1,0:T(8,128)(2,1)S(1)}, u32[]{:S(2)}, u32[]{:S(2)}) collective-permute-start(bf16[16,352,128]{2,1,0:T(8,128)(2,1)S(1)} %get-tuple-element.212), channel_id=1, source_target_pairs={{0,32},{1,97},{2,34},{3,99},{4,36},{5,101},{6,38},{7,103},{8,40},{... | collective-permute-start | bytes 4325384 | tf_op jit(solution)/shard_map/ppermute | solution.py:472
  8.6 38.3 %collective-permute-start.61 = (bf16[16,336,128]{2,1,0:T(8,128)(2,1)}, bf16[16,336,128]{2,1,0:T(8,128)(2,1)}, u32[]{:S(2)}, u32[]{:S(2)}) collective-permute-start(bf16[16,336,128]{2,1,0:T(8,128)(2,1)} %get-tuple-element.213), channel_id=1, source_target_pairs={{0,8},{1,25},{2,10},{3,27},{4,12},{5,29},{6,14},{7,31},{8,16},{9,1... | collective-permute-start | bytes 4128776 | tf_op jit(solution)/shard_map/ppermute | solution.py:472
  12.4 34.6 %collective-permute-start.62 = (bf16[16,336,128]{2,1,0:T(8,128)(2,1)}, bf16[16,336,128]{2,1,0:T(8,128)(2,1)}, u32[]{:S(2)}, u32[]{:S(2)}) collective-permute-start(bf16[16,336,128]{2,1,0:T(8,128)(2,1)} %get-tuple-element.214), channel_id=1, source_target_pairs={{0,2},{1,7},{2,4},{3,1},{4,6},{5,3},{6,0},{7,5},{8,10},{9,15},{10,... | collective-permute-start | bytes 4128776 | tf_op jit(solution)/shard_map/ppermute | solution.py:472
  16.2 17.7 %all-to-all-start = ((s32[128,1,128]{2,1,0:T(1,128)}), s32[128,1,128]{2,1,0:T(1,128)S(1)}, u32[]{:S(2)}, u32[]{:S(2)}) async-start(s32[128,1,128]{2,1,0:T(1,128)} %broadcast_in_dim.20), calls=%async_computation | async-start | bytes 131072 | tf_op jit(solution)/shard_map/all_to_all | solution.py:528
  40.0 17.8 %collective-permute-start.70 = (bf16[16,336,128]{2,1,0:T(8,128)(2,1)}, bf16[16,336,128]{2,1,0:T(8,128)(2,1)}, u32[]{:S(2)}, u32[]{:S(2)}) collective-permute-start(bf16[16,336,128]{2,1,0:T(8,128)(2,1)} %get-tuple-element.221), channel_id=1, source_target_pairs={{0,8},{1,25},{2,10},{3,27},{4,12},{5,29},{6,14},{7,31},{8,16},{9,1... | collective-permute-start | bytes 4128776 | tf_op jit(solution)/shard_map/ppermute | solution.py:472
  40.8 18.5 %collective-permute-start.75 = (bf16[16,336,128]{2,1,0:T(8,128)(2,1)}, bf16[16,336,128]{2,1,0:T(8,128)(2,1)}, u32[]{:S(2)}, u32[]{:S(2)}) collective-permute-start(bf16[16,336,128]{2,1,0:T(8,128)(2,1)} %get-tuple-element.223), channel_id=1, source_target_pairs={{0,2},{1,7},{2,4},{3,1},{4,6},{5,3},{6,0},{7,5},{8,10},{9,15},{10,... | collective-permute-start | bytes 4128776 | tf_op jit(solution)/shard_map/ppermute | solution.py:472
  47.0 25.6 %collective-permute-start.73 = (bf16[16,336,128]{2,1,0:T(8,128)(2,1)}, bf16[16,336,128]{2,1,0:T(8,128)(2,1)}, u32[]{:S(2)}, u32[]{:S(2)}) collective-permute-start(bf16[16,336,128]{2,1,0:T(8,128)(2,1)} %collective-permute-done.61), channel_id=1, source_target_pairs={{0,8},{1,25},{2,10},{3,27},{4,12},{5,29},{6,14},{7,31},{8,16},{9,1... | collective-permute-start | bytes 4128776 | tf_op jit(solution)/shard_map/ppermute | solution.py:472
  47.6 27.7 %collective-permute-start.71 = (bf16[16,336,128]{2,1,0:T(8,128)(2,1)}, bf16[16,336,128]{2,1,0:T(8,128)(2,1)S(1)}, u32[]{:S(2)}, u32[]{:S(2)}) collective-permute-start(bf16[16,336,128]{2,1,0:T(8,128)(2,1)} %collective-permute-done.61), channel_id=1, source_target_pairs={{0,1},{1,0},{2,3},{3,2},{4,5},{5,4},{6,7},{7,6},{8,9},{9,8},{10,11... | collective-permute-start | bytes 4128776 | tf_op jit(solution)/shard_map/ppermute | solution.py:476
  47.6 27.7 %collective-permute-start.78 = (bf16[16,336,128]{2,1,0:T(8,128)(2,1)}, bf16[16,336,128]{2,1,0:T(8,128)(2,1)}, u32[]{:S(2)}, u32[]{:S(2)}) collective-permute-start(bf16[16,336,128]{2,1,0:T(8,128)(2,1)} %collective-permute-done.62), channel_id=1, source_target_pairs={{0,2},{1,7},{2,4},{3,1},{4,6},{5,3},{6,0},{7,5},{8,10},{9,15},{10,... | collective-permute-start | bytes 4128776 | tf_op jit(solution)/shard_map/ppermute | solution.py:472
  57.8 18.5 %collective-permute-start.65 = (bf16[16,352,128]{2,1,0:T(8,128)(2,1)}, bf16[16,352,128]{2,1,0:T(8,128)(2,1)}, u32[]{:S(2)}, u32[]{:S(2)}) collective-permute-start(bf16[16,352,128]{2,1,0:T(8,128)(2,1)} %get-tuple-element.219), channel_id=1, source_target_pairs={{0,32},{1,97},{2,34},{3,99},{4,36},{5,101},{6,38},{7,103},{8,40},{... | collective-permute-start | bytes 4325384 | tf_op jit(solution)/shard_map/ppermute | solution.py:472
  59.3 32.5 %collective-permute-start.68 = (bf16[16,352,128]{2,1,0:T(8,128)(2,1)S(1)}, bf16[16,352,128]{2,1,0:T(8,128)(2,1)}, u32[]{:S(2)}, u32[]{:S(2)}) collective-permute-start(bf16[16,352,128]{2,1,0:T(8,128)(2,1)S(1)} %collective-permute-done.60), channel_id=1, source_target_pairs={{0,32},{1,97},{2,34},{3,99},{4,36},{5,101},{6,38},{7,103},{8,40},{... | collective-permute-start | bytes 4325384 | tf_op jit(solution)/shard_map/ppermute | solution.py:472
  72.5 24.1 %collective-permute-start.66 = (bf16[16,352,128]{2,1,0:T(8,128)(2,1)S(1)}, bf16[16,352,128]{2,1,0:T(8,128)(2,1)S(1)}, u32[]{:S(2)}, u32[]{:S(2)}) collective-permute-start(bf16[16,352,128]{2,1,0:T(8,128)(2,1)S(1)} %collective-permute-done.60), channel_id=1, source_target_pairs={{0,1},{1,0},{2,3},{3,2},{4,5},{5,4},{6,7},{7,6},{8,9},{9,8},{10,11... | collective-permute-start | bytes 4325384 | tf_op jit(solution)/shard_map/ppermute | solution.py:476
  75.3 21.2 %collective-permute-start.76 = (bf16[16,336,128]{2,1,0:T(8,128)(2,1)}, bf16[16,336,128]{2,1,0:T(8,128)(2,1)S(1)}, u32[]{:S(2)}, u32[]{:S(2)}) collective-permute-start(bf16[16,336,128]{2,1,0:T(8,128)(2,1)} %collective-permute-done.62), channel_id=1, source_target_pairs={{0,1},{1,0},{2,3},{3,2},{4,5},{5,4},{6,7},{7,6},{8,9},{9,8},{10,11... | collective-permute-start | bytes 4128776 | tf_op jit(solution)/shard_map/ppermute | solution.py:476
  75.4 22.8 %collective-permute-start.72 = (bf16[16,336,128]{2,1,0:T(8,128)(2,1)}, bf16[16,336,128]{2,1,0:T(8,128)(2,1)S(1)}, u32[]{:S(2)}, u32[]{:S(2)}) collective-permute-start(bf16[16,336,128]{2,1,0:T(8,128)(2,1)} %collective-permute-done.70), channel_id=1, source_target_pairs={{0,1},{1,0},{2,3},{3,2},{4,5},{5,4},{6,7},{7,6},{8,9},{9,8},{10,11... | collective-permute-start | bytes 4128776 | tf_op jit(solution)/shard_map/ppermute | solution.py:476
  76.3 29.4 %collective-permute-start.67 = (bf16[16,352,128]{2,1,0:T(8,128)(2,1)}, bf16[16,352,128]{2,1,0:T(8,128)(2,1)}, u32[]{:S(2)}, u32[]{:S(2)}) collective-permute-start(bf16[16,352,128]{2,1,0:T(8,128)(2,1)} %collective-permute-done.65), channel_id=1, source_target_pairs={{0,1},{1,0},{2,3},{3,2},{4,5},{5,4},{6,7},{7,6},{8,9},{9,8},{10,11... | collective-permute-start | bytes 4325384 | tf_op jit(solution)/shard_map/ppermute | solution.py:476
  91.7 13.9 %collective-permute-start.69 = (bf16[16,352,128]{2,1,0:T(8,128)(2,1)}, bf16[16,352,128]{2,1,0:T(8,128)(2,1)}, u32[]{:S(2)}, u32[]{:S(2)}) collective-permute-start(bf16[16,352,128]{2,1,0:T(8,128)(2,1)} %collective-permute-done.68), channel_id=1, source_target_pairs={{0,1},{1,0},{2,3},{3,2},{4,5},{5,4},{6,7},{7,6},{8,9},{9,8},{10,11... | collective-permute-start | bytes 4325384 | tf_op jit(solution)/shard_map/ppermute | solution.py:476
  99.3 6.3 %collective-permute-start.79 = (bf16[16,336,128]{2,1,0:T(8,128)(2,1)}, bf16[16,336,128]{2,1,0:T(8,128)(2,1)}, u32[]{:S(2)}, u32[]{:S(2)}) collective-permute-start(bf16[16,336,128]{2,1,0:T(8,128)(2,1)} %collective-permute-done.78), channel_id=1, source_target_pairs={{0,1},{1,0},{2,3},{3,2},{4,5},{5,4},{6,7},{7,6},{8,9},{9,8},{10,11... | collective-permute-start | bytes 4128776 | tf_op jit(solution)/shard_map/ppermute | solution.py:476
  125.1 23.2 %collective-permute-start.37 = (bf16[22,336,128]{2,1,0:T(8,128)(2,1)S(1)}, bf16[22,336,128]{2,1,0:T(8,128)(2,1)}, u32[]{:S(2)}, u32[]{:S(2)}) collective-permute-start(bf16[22,336,128]{2,1,0:T(8,128)(2,1)S(1)} %pack.37), channel_id=1, source_target_pairs={{0,2},{1,7},{2,4},{3,1},{4,6},{5,3},{6,0},{7,5},{8,10},{9,15},{10,... | collective-permute-start | bytes 5677064 | tf_op jit(solution)/shard_map/cond/branch_1_fun/ppermute | solution.py:472
  131.5 77.6 %collective-permute-start.30 = (bf16[44,352,128]{2,1,0:T(8,128)(2,1)S(1)}, bf16[44,352,128]{2,1,0:T(8,128)(2,1)S(1)}, u32[]{:S(2)}, u32[]{:S(2)}) collective-permute-start(bf16[44,352,128]{2,1,0:T(8,128)(2,1)S(1)} %pack.39), channel_id=1, source_target_pairs={{0,8},{1,25},{2,10},{3,27},{4,12},{5,29},{6,14},{7,31},{8,16},{9,1... | collective-permute-start | bytes 11894792 | tf_op jit(solution)/shard_map/cond/branch_1_fun/ppermute | solution.py:472
  133.2 23.0 %collective-permute-start.42 = (bf16[22,336,128]{2,1,0:T(8,128)(2,1)S(1)}, bf16[22,336,128]{2,1,0:T(8,128)(2,1)S(1)}, u32[]{:S(2)}, u32[]{:S(2)}) collective-permute-start(bf16[22,336,128]{2,1,0:T(8,128)(2,1)S(1)} %pack.38), channel_id=1, source_target_pairs={{0,32},{1,97},{2,34},{3,99},{4,36},{5,101},{6,38},{7,103},{8,40},{... | collective-permute-start | bytes 5677064 | tf_op jit(solution)/shard_map/cond/branch_1_fun/ppermute | solution.py:472
  133.2 64.8 %collective-permute-start.32 = (bf16[22,352,128]{2,1,0:T(8,128)(2,1)S(1)}, bf16[22,352,128]{2,1,0:T(8,128)(2,1)S(1)}, u32[]{:S(2)}, u32[]{:S(2)}) collective-permute-start(bf16[22,352,128]{2,1,0:T(8,128)(2,1)S(1)} %pack.36), channel_id=1, source_target_pairs={{0,8},{1,25},{2,10},{3,27},{4,12},{5,29},{6,14},{7,31},{8,16},{9,1... | collective-permute-start | bytes 5947400 | tf_op jit(solution)/shard_map/cond/branch_1_fun/ppermute | solution.py:472
  139.3 72.2 %collective-permute-start.35 = (bf16[44,336,128]{2,1,0:T(8,128)(2,1)S(1)}, bf16[44,336,128]{2,1,0:T(8,128)(2,1)S(1)}, u32[]{:S(2)}, u32[]{:S(2)}) collective-permute-start(bf16[44,336,128]{2,1,0:T(8,128)(2,1)S(1)} %pack.41), channel_id=1, source_target_pairs={{0,2},{1,7},{2,4},{3,1},{4,6},{5,3},{6,0},{7,5},{8,10},{9,15},{10,... | collective-permute-start | bytes 11354120 | tf_op jit(solution)/shard_map/cond/branch_1_fun/ppermute | solution.py:472
  148.2 77.3 %collective-permute-start.40 = (bf16[44,336,128]{2,1,0:T(8,128)(2,1)S(1)}, bf16[44,336,128]{2,1,0:T(8,128)(2,1)S(1)}, u32[]{:S(2)}, u32[]{:S(2)}) collective-permute-start(bf16[44,336,128]{2,1,0:T(8,128)(2,1)S(1)} %pack.43), channel_id=1, source_target_pairs={{0,32},{1,97},{2,34},{3,99},{4,36},{5,101},{6,38},{7,103},{8,40},{... | collective-permute-start | bytes 11354120 | tf_op jit(solution)/shard_map/cond/branch_1_fun/ppermute | solution.py:472
  156.2 52.8 %collective-permute-start.38 = (bf16[22,336,128]{2,1,0:T(8,128)(2,1)}, bf16[22,336,128]{2,1,0:T(8,128)(2,1)S(1)}, u32[]{:S(2)}, u32[]{:S(2)}) collective-permute-start(bf16[22,336,128]{2,1,0:T(8,128)(2,1)} %collective-permute-done.37), channel_id=1, source_target_pairs={{0,2},{1,7},{2,4},{3,1},{4,6},{5,3},{6,0},{7,5},{8,10},{9,15},{10,... | collective-permute-start | bytes 5677064 | tf_op jit(solution)/shard_map/cond/branch_1_fun/ppermute | solution.py:472
  198.0 23.0 %collective-permute-start.43 = (bf16[22,336,128]{2,1,0:T(8,128)(2,1)S(1)}, bf16[22,336,128]{2,1,0:T(8,128)(2,1)S(1)}, u32[]{:S(2)}, u32[]{:S(2)}) collective-permute-start(bf16[22,336,128]{2,1,0:T(8,128)(2,1)S(1)} %collective-permute-done.42), channel_id=1, source_target_pairs={{0,32},{1,97},{2,34},{3,99},{4,36},{5,101},{6,38},{7,103},{8,40},{... | collective-permute-start | bytes 5677064 | tf_op jit(solution)/shard_map/cond/branch_1_fun/ppermute | solution.py:472
  209.0 24.0 %collective-permute-start.33 = (bf16[22,352,128]{2,1,0:T(8,128)(2,1)S(1)}, bf16[22,352,128]{2,1,0:T(8,128)(2,1)S(1)}, u32[]{:S(2)}, u32[]{:S(2)}) collective-permute-start(bf16[22,352,128]{2,1,0:T(8,128)(2,1)S(1)} %collective-permute-done.32), channel_id=1, source_target_pairs={{0,8},{1,25},{2,10},{3,27},{4,12},{5,29},{6,14},{7,31},{8,16},{9,1... | collective-permute-start | bytes 5947400 | tf_op jit(solution)/shard_map/cond/branch_1_fun/ppermute | solution.py:472
  209.1 40.0 %collective-permute-start.31 = (bf16[44,352,128]{2,1,0:T(8,128)(2,1)S(1)}, bf16[44,352,128]{2,1,0:T(8,128)(2,1)S(1)}, u32[]{:S(2)}, u32[]{:S(2)}) collective-permute-start(bf16[44,352,128]{2,1,0:T(8,128)(2,1)S(1)} %collective-permute-done.30.refs_8_), channel_id=1, source_target_pairs={{0,1},{1,0},{2,3},{3,2},{4,5},{5,4},{6,7},{7,6},{8,9},{9,8},{10,11... | collective-permute-start | bytes 11894792 | tf_op jit(solution)/shard_map/cond/branch_1_fun/ppermute | solution.py:476
  211.5 26.0 %collective-permute-start.36 = (bf16[44,336,128]{2,1,0:T(8,128)(2,1)S(1)}, bf16[44,336,128]{2,1,0:T(8,128)(2,1)S(1)}, u32[]{:S(2)}, u32[]{:S(2)}) collective-permute-start(bf16[44,336,128]{2,1,0:T(8,128)(2,1)S(1)} %collective-permute-done.35.refs_8_.refs_24_), channel_id=1, source_target_pairs={{0,1},{1,0},{2,3},{3,2},{4,5},{5,4},{6,7},{7,6},{8,9},{9,8},{10,11... | collective-permute-start | bytes 11354120 | tf_op jit(solution)/shard_map/cond/branch_1_fun/ppermute | solution.py:476
  221.0 16.4 %collective-permute-start.39 = (bf16[22,336,128]{2,1,0:T(8,128)(2,1)S(1)}, bf16[22,336,128]{2,1,0:T(8,128)(2,1)S(1)}, u32[]{:S(2)}, u32[]{:S(2)}) collective-permute-start(bf16[22,336,128]{2,1,0:T(8,128)(2,1)S(1)} %collective-permute-done.38.refs_10_.refs_26_), channel_id=1, source_target_pairs={{0,1},{1,0},{2,3},{3,2},{4,5},{5,4},{6,7},{7,6},{8,9},{9,8},{10,11... | collective-permute-start | bytes 5677064 | tf_op jit(solution)/shard_map/cond/branch_1_fun/ppermute | solution.py:476
  225.5 18.2 %collective-permute-start.41 = (bf16[44,336,128]{2,1,0:T(8,128)(2,1)S(1)}, bf16[44,336,128]{2,1,0:T(8,128)(2,1)S(1)}, u32[]{:S(2)}, u32[]{:S(2)}) collective-permute-start(bf16[44,336,128]{2,1,0:T(8,128)(2,1)S(1)} %collective-permute-done.40.refs_8_.refs_40_), channel_id=1, source_target_pairs={{0,1},{1,0},{2,3},{3,2},{4,5},{5,4},{6,7},{7,6},{8,9},{9,8},{10,11... | collective-permute-start | bytes 11354120 | tf_op jit(solution)/shard_map/cond/branch_1_fun/ppermute | solution.py:476
  232.9 16.2 %collective-permute-start.34 = (bf16[22,352,128]{2,1,0:T(8,128)(2,1)S(1)}, bf16[22,352,128]{2,1,0:T(8,128)(2,1)S(1)}, u32[]{:S(2)}, u32[]{:S(2)}) collective-permute-start(bf16[22,352,128]{2,1,0:T(8,128)(2,1)S(1)} %collective-permute-done.33.refs_10_), channel_id=1, source_target_pairs={{0,1},{1,0},{2,3},{3,2},{4,5},{5,4},{6,7},{7,6},{8,9},{9,8},{10,11... | collective-permute-start | bytes 5947400 | tf_op jit(solution)/shard_map/cond/branch_1_fun/ppermute | solution.py:476
  255.0 25.8 %collective-permute-start.52 = (bf16[24,336,128]{2,1,0:T(8,128)(2,1)}, bf16[24,336,128]{2,1,0:T(8,128)(2,1)}, u32[]{:S(2)}, u32[]{:S(2)}) collective-permute-start(bf16[24,336,128]{2,1,0:T(8,128)(2,1)} %pack.42), channel_id=1, source_target_pairs={{0,32},{1,97},{2,34},{3,99},{4,36},{5,101},{6,38},{7,103},{8,40},{... | collective-permute-start | bytes 6193160 | tf_op jit(solution)/shard_map/cond/branch_1_fun/ppermute | solution.py:472
  264.5 82.1 %collective-permute-start.45 = (bf16[48,352,128]{2,1,0:T(8,128)(2,1)}, bf16[48,352,128]{2,1,0:T(8,128)(2,1)}, u32[]{:S(2)}, u32[]{:S(2)}) collective-permute-start(bf16[48,352,128]{2,1,0:T(8,128)(2,1)} %pack.45), channel_id=1, source_target_pairs={{0,2},{1,7},{2,4},{3,1},{4,6},{5,3},{6,0},{7,5},{8,10},{9,15},{10,... | collective-permute-start | bytes 12976136 | tf_op jit(solution)/shard_map/cond/branch_1_fun/ppermute | solution.py:472
  264.5 25.2 %collective-permute-start.57 = (bf16[24,336,128]{2,1,0:T(8,128)(2,1)}, bf16[24,336,128]{2,1,0:T(8,128)(2,1)}, u32[]{:S(2)}, u32[]{:S(2)}) collective-permute-start(bf16[24,336,128]{2,1,0:T(8,128)(2,1)} %pack.44), channel_id=1, source_target_pairs={{0,8},{1,25},{2,10},{3,27},{4,12},{5,29},{6,14},{7,31},{8,16},{9,1... | collective-permute-start | bytes 6193160 | tf_op jit(solution)/shard_map/cond/branch_1_fun/ppermute | solution.py:472
  264.8 72.3 %collective-permute-start.47 = (bf16[24,352,128]{2,1,0:T(8,128)(2,1)}, bf16[24,352,128]{2,1,0:T(8,128)(2,1)}, u32[]{:S(2)}, u32[]{:S(2)}) collective-permute-start(bf16[24,352,128]{2,1,0:T(8,128)(2,1)} %pack.40), channel_id=1, source_target_pairs={{0,2},{1,7},{2,4},{3,1},{4,6},{5,3},{6,0},{7,5},{8,10},{9,15},{10,... | collective-permute-start | bytes 6488072 | tf_op jit(solution)/shard_map/cond/branch_1_fun/ppermute | solution.py:472
  271.8 95.3 %collective-permute-start.50 = (bf16[48,336,128]{2,1,0:T(8,128)(2,1)S(1)}, bf16[48,336,128]{2,1,0:T(8,128)(2,1)}, u32[]{:S(2)}, u32[]{:S(2)}) collective-permute-start(bf16[48,336,128]{2,1,0:T(8,128)(2,1)S(1)} %pack.46), channel_id=1, source_target_pairs={{0,32},{1,97},{2,34},{3,99},{4,36},{5,101},{6,38},{7,103},{8,40},{... | collective-permute-start | bytes 12386312 | tf_op jit(solution)/shard_map/cond/branch_1_fun/ppermute | solution.py:472
  280.8 86.4 %collective-permute-start.55 = (bf16[48,336,128]{2,1,0:T(8,128)(2,1)S(1)}, bf16[48,336,128]{2,1,0:T(8,128)(2,1)S(1)}, u32[]{:S(2)}, u32[]{:S(2)}) collective-permute-start(bf16[48,336,128]{2,1,0:T(8,128)(2,1)S(1)} %pack.47), channel_id=1, source_target_pairs={{0,8},{1,25},{2,10},{3,27},{4,12},{5,29},{6,14},{7,31},{8,16},{9,1... | collective-permute-start | bytes 12386312 | tf_op jit(solution)/shard_map/cond/branch_1_fun/ppermute | solution.py:472
  289.8 56.8 %collective-permute-start.53 = (bf16[24,336,128]{2,1,0:T(8,128)(2,1)}, bf16[24,336,128]{2,1,0:T(8,128)(2,1)S(1)}, u32[]{:S(2)}, u32[]{:S(2)}) collective-permute-start(bf16[24,336,128]{2,1,0:T(8,128)(2,1)} %collective-permute-done.52), channel_id=1, source_target_pairs={{0,32},{1,97},{2,34},{3,99},{4,36},{5,101},{6,38},{7,103},{8,40},{... | collective-permute-start | bytes 6193160 | tf_op jit(solution)/shard_map/cond/branch_1_fun/ppermute | solution.py:472
  337.1 25.0 %collective-permute-start.58 = (bf16[24,336,128]{2,1,0:T(8,128)(2,1)}, bf16[24,336,128]{2,1,0:T(8,128)(2,1)S(1)}, u32[]{:S(2)}, u32[]{:S(2)}) collective-permute-start(bf16[24,336,128]{2,1,0:T(8,128)(2,1)} %collective-permute-done.57), channel_id=1, source_target_pairs={{0,8},{1,25},{2,10},{3,27},{4,12},{5,29},{6,14},{7,31},{8,16},{9,1... | collective-permute-start | bytes 6193160 | tf_op jit(solution)/shard_map/cond/branch_1_fun/ppermute | solution.py:472
  346.5 26.1 %collective-permute-start.48 = (bf16[24,352,128]{2,1,0:T(8,128)(2,1)}, bf16[24,352,128]{2,1,0:T(8,128)(2,1)S(1)}, u32[]{:S(2)}, u32[]{:S(2)}) collective-permute-start(bf16[24,352,128]{2,1,0:T(8,128)(2,1)} %collective-permute-done.47), channel_id=1, source_target_pairs={{0,2},{1,7},{2,4},{3,1},{4,6},{5,3},{6,0},{7,5},{8,10},{9,15},{10,... | collective-permute-start | bytes 6488072 | tf_op jit(solution)/shard_map/cond/branch_1_fun/ppermute | solution.py:472
  346.5 42.3 %collective-permute-start.46 = (bf16[48,352,128]{2,1,0:T(8,128)(2,1)}, bf16[48,352,128]{2,1,0:T(8,128)(2,1)S(1)}, u32[]{:S(2)}, u32[]{:S(2)}) collective-permute-start(bf16[48,352,128]{2,1,0:T(8,128)(2,1)} %collective-permute-done.45.refs_12_), channel_id=1, source_target_pairs={{0,1},{1,0},{2,3},{3,2},{4,5},{5,4},{6,7},{7,6},{8,9},{9,8},{10,11... | collective-permute-start | bytes 12976136 | tf_op jit(solution)/shard_map/cond/branch_1_fun/ppermute | solution.py:476
  362.1 15.2 %collective-permute-start.54 = (bf16[24,336,128]{2,1,0:T(8,128)(2,1)S(1)}, bf16[24,336,128]{2,1,0:T(8,128)(2,1)S(1)}, u32[]{:S(2)}, u32[]{:S(2)}) collective-permute-start(bf16[24,336,128]{2,1,0:T(8,128)(2,1)S(1)} %collective-permute-done.53.refs_30_), channel_id=1, source_target_pairs={{0,1},{1,0},{2,3},{3,2},{4,5},{5,4},{6,7},{7,6},{8,9},{9,8},{10,11... | collective-permute-start | bytes 6193160 | tf_op jit(solution)/shard_map/cond/branch_1_fun/ppermute | solution.py:476
  367.1 21.6 %collective-permute-start.51 = (bf16[48,336,128]{2,1,0:T(8,128)(2,1)}, bf16[48,336,128]{2,1,0:T(8,128)(2,1)S(1)}, u32[]{:S(2)}, u32[]{:S(2)}) collective-permute-start(bf16[48,336,128]{2,1,0:T(8,128)(2,1)} %collective-permute-done.50.refs_28_), channel_id=1, source_target_pairs={{0,1},{1,0},{2,3},{3,2},{4,5},{5,4},{6,7},{7,6},{8,9},{9,8},{10,11... | collective-permute-start | bytes 12386312 | tf_op jit(solution)/shard_map/cond/branch_1_fun/ppermute | solution.py:476
  367.2 21.5 %collective-permute-start.56 = (bf16[48,336,128]{2,1,0:T(8,128)(2,1)S(1)}, bf16[48,336,128]{2,1,0:T(8,128)(2,1)S(1)}, u32[]{:S(2)}, u32[]{:S(2)}) collective-permute-start(bf16[48,336,128]{2,1,0:T(8,128)(2,1)S(1)} %collective-permute-done.55.refs_44_), channel_id=1, source_target_pairs={{0,1},{1,0},{2,3},{3,2},{4,5},{5,4},{6,7},{7,6},{8,9},{9,8},{10,11... | collective-permute-start | bytes 12386312 | tf_op jit(solution)/shard_map/cond/branch_1_fun/ppermute | solution.py:476
  372.6 16.1 %collective-permute-start.49 = (bf16[24,352,128]{2,1,0:T(8,128)(2,1)S(1)}, bf16[24,352,128]{2,1,0:T(8,128)(2,1)S(1)}, u32[]{:S(2)}, u32[]{:S(2)}) collective-permute-start(bf16[24,352,128]{2,1,0:T(8,128)(2,1)S(1)} %collective-permute-done.48.refs_14_), channel_id=1, source_target_pairs={{0,1},{1,0},{2,3},{3,2},{4,5},{5,4},{6,7},{7,6},{8,9},{9,8},{10,11... | collective-permute-start | bytes 6488072 | tf_op jit(solution)/shard_map/cond/branch_1_fun/ppermute | solution.py:476
  377.3 11.4 %collective-permute-start.59 = (bf16[24,336,128]{2,1,0:T(8,128)(2,1)S(1)}, bf16[24,336,128]{2,1,0:T(8,128)(2,1)S(1)}, u32[]{:S(2)}, u32[]{:S(2)}) collective-permute-start(bf16[24,336,128]{2,1,0:T(8,128)(2,1)S(1)} %collective-permute-done.58.refs_46_), channel_id=1, source_target_pairs={{0,1},{1,0},{2,3},{3,2},{4,5},{5,4},{6,7},{7,6},{8,9},{9,8},{10,11... | collective-permute-start | bytes 6193160 | tf_op jit(solution)/shard_map/cond/branch_1_fun/ppermute | solution.py:476
  (52 other events, 1272.1 us)

commit v3 on v2

--- a/solution.py
+++ b/solution.py
@@ -27,21 +27,18 @@
         go(refs[0])
         return
     half = len(refs) // 2
-
-    @pl.when(which < half)
-    def _():
-        pick(which, refs[:half], go)
-
-    @pl.when(which >= half)
-    def _():
-        pick(which - half, refs[half:], go)
+    lax.cond(
+        which < half,
+        lambda: pick(which, refs[:half], go),
+        lambda: pick(which - half, refs[half:], go),
+    )
 
 
 def attend_kernel(pieces, counts, spans, table, q_ref, nk_ref, nv_ref, *refs):
     total = sum(counts)
     sources = refs[:total]
     out_ref, k_buf, v_buf, nv_buf, sems = refs[-5:]
-    heads, first, many = spans
+    heads, first, many, unroll = spans
     step = pl.program_id(0)
     steps = pl.num_programs(0)
     scale = HD ** -0.5 * 1.4426950408889634
@@ -90,12 +87,13 @@
 
     half = 256
     dims = (((1,), (1,)), ((), ()))
-    tiles = [(a, part) for a in range(GROUP) for part in range(BLOCK // half)]
-
-    def score(n):
-        a, part = tiles[n]
+    parts = BLOCK // half
+    head_lanes = lambda a: pl.ds(a * HD if unroll else pl.multiple_of(a * HD, HD), HD)
+
+    def score(tile):
+        a, part = tile
         keys = half * (part + 1)
-        q = q_ref[pl.ds(part * half, half), pl.ds(a * HD, HD)]
+        q = q_ref[pl.ds(part * half, half), head_lanes(a)]
         near = lax.dot_general(q, nk_ref[:keys, :], dims, preferred_element_type=jnp.float32)
         seen = lax.broadcasted_iota(jnp.int32, (half, keys), 1) <= (
             lax.broadcasted_iota(jnp.int32, (half, keys), 0) + part * half
@@ -105,8 +103,8 @@
             out.append(lax.dot_general(q, k_buf[slot, j], dims, preferred_element_type=jnp.float32))
         return out
 
-    def finish(n, scores):
-        a, part = tiles[n]
+    def finish(tile, scores):
+        a, part = tile
         keys = half * (part + 1)
         wide = None
         for x in scores:
@@ -121,18 +119,27 @@
             w = jnp.exp2(x * scale - top).astype(jnp.bfloat16)
             y = jnp.dot(w, v, preferred_element_type=jnp.float32)
             acc = y if acc is None else acc + y
-        out_ref[pl.ds(part * half, half), pl.ds(a * HD, HD)] = (
+        out_ref[pl.ds(part * half, half), head_lanes(a)] = (
             acc[:, :HD] / acc[:, HD:]
         ).astype(jnp.bfloat16)
 
-    held = score(0)
-    for n in range(len(tiles)):
-        later = score(n + 1) if n + 1 < len(tiles) else None
-        finish(n, held)
-        held = later
-
-
-def attend(queries, span_keys, span_values, table, pieces, groups, first, many, before=None):
+    def chain(tiles):
+        held = score(tiles[0])
+        for n, tile in enumerate(tiles):
+            later = score(tiles[n + 1]) if n + 1 < len(tiles) else None
+            finish(tile, held)
+            held = later
+
+    if unroll:
+        chain([(a, part) for a in range(GROUP) for part in range(parts)])
+    else:
+
+        @pl.loop(0, GROUP)
+        def _(a):
+            chain([(a, part) for part in range(parts)])
+
+
+def attend(queries, span_keys, span_values, table, pieces, groups, first, many, unroll, before=None):
     tokens, width = queries.shape
     heads = span_keys.shape[1] // HD
     blocks = tokens // BLOCK
@@ -143,7 +150,7 @@
     pairs = 2 * tokens * many * GROUP * BLOCK * (TOPK + 1)
     extra = [] if before is None else [before]
     return pl.pallas_call(
-        functools.partial(attend_kernel, pieces, counts, (heads, first, many)),
+        functools.partial(attend_kernel, pieces, counts, (heads, first, many, unroll)),
         out_shape=jax.ShapeDtypeStruct((tokens, width), jnp.bfloat16),
         grid_spec=pltpu.PrefetchScalarGridSpec(
             num_scalar_prefetch=1,
@@ -153,7 +160,7 @@
                 pl.BlockSpec((BLOCK, HD), place),
                 pl.BlockSpec((BLOCK, HD), place),
             ]
-            + [pl.BlockSpec(memory_space=pltpu.HBM)] * (len(flat) + len(extra)),
+            + [pl.BlockSpec(memory_space=pl.ANY)] * (len(flat) + len(extra)),
             out_specs=pl.BlockSpec((BLOCK, GROUP * HD), place),
             scratch_shapes=[
                 pltpu.VMEM((2, TOPK, BLOCK, HD), jnp.bfloat16),
@@ -164,7 +171,7 @@
         ),
         input_output_aliases={} if before is None else {4 + len(flat): 0},
         compiler_params=pltpu.CompilerParams(
-            dimension_semantics=("arbitrary",), vmem_limit_bytes=40 * 1024 * 1024
+            dimension_semantics=("arbitrary",), vmem_limit_bytes=20 * 1024 * 1024
         ),
         cost_estimate=pl.CostEstimate(
             flops=4 * HD * pairs,
@@ -451,10 +458,10 @@
         functools.partial(pack_kernel, row, first, count, len(sources)),
         out_shape=jax.ShapeDtypeStruct((count, rows, HD), jnp.bfloat16),
         in_specs=[pl.BlockSpec(memory_space=pltpu.SMEM)]
-        + [pl.BlockSpec(memory_space=pltpu.HBM)] * len(sources),
+        + [pl.BlockSpec(memory_space=pl.ANY)] * len(sources),
         out_specs=pl.BlockSpec(memory_space=pltpu.VMEM),
         scratch_shapes=[pltpu.SemaphoreType.DMA],
-        compiler_params=pltpu.CompilerParams(vmem_limit_bytes=24 * 1024 * 1024),
+        compiler_params=pltpu.CompilerParams(vmem_limit_bytes=12 * 1024 * 1024),
         name="pack",
     )(table, *sources)
 
@@ -478,11 +485,15 @@
 
 def hop(pools, table, row, axis_of, cap):
     half = cap // 2
-    packed = [pack(table, t * 8 + row, cap, half, pools[t]) for t in range(3)]
-    table, packed = lax.optimization_barrier((table, packed))
-    through = [onward(packed[t], axis_of(t)) for t in range(3)]
-    direct = [onward(pack(table, t * 8 + row, 0, cap, pools[t]), axis_of(t)) for t in range(3)]
+    first = [pack(table, t * 8 + row, cap, half, pools[t]) for t in range(3)]
+    through = [onward(first[t], axis_of(t)) for t in range(3)]
+    table, _ = lax.optimization_barrier((table, first))
+    second = [pack(table, t * 8 + row, 0, cap, pools[t]) for t in range(3)]
+    second, through = lax.optimization_barrier((second, through))
+    direct = [onward(second[t], axis_of(t)) for t in range(3)]
+    through, direct = lax.optimization_barrier((through, direct))
     passed = [onward(through[t], axis_of(t)) for t in range(3)]
+    passed = lax.optimization_barrier(passed)
     return [[direct[t], swap(direct[t]), passed[t], swap(passed[t])] for t in range(3)]
 
 
@@ -490,9 +501,7 @@
     return [sum((x[t] for x in lists), []) for t in range(3)]
 
 
-def route(cut, caps2, caps3, splits, queries, span_keys, span_values, pools, place, wanted, requests, table):
-    if caps2 != FAST[1]:
-        table = make_plan(cut, caps2, caps3, place, wanted, requests)
+def route(cut, caps2, caps3, splits, queries, span_keys, span_values, past_keys, past_values, pools, place, wanted, requests, table):
     side = lambda t: (t + 1) % 3
     last = lambda t: (t + 2) % 3
     starts = (0, ROWS[0], ROWS[0] + ROWS[1])
@@ -507,12 +516,28 @@
     out = None
     for ranges, found in zip(splits, groups):
         for first, many in ranges:
-            out = attend(queries, span_keys, span_values, table, pieces, found, first, many, out)
+            out = attend(queries, span_keys, span_values, table, pieces, found, first, many, True, out)
     return out
 
 
 FAST = (8, (44, 0), (48, 0), (((0, 8),),))
-SAFE = (8, (64, 0), (64, 0), (((0, 8),),))
+
+
+def dense(queries, span_keys, span_values, past_keys, past_values, pools, place, wanted, requests, table):
+    me = lax.axis_index("seq")
+    heads = span_keys.shape[1] // HD
+    item = jnp.maximum(jnp.take(wanted, me, axis=1) - 1, 0)
+    stacked = jnp.concatenate(
+        [
+            x.reshape(-1, BLOCK, heads, HD).transpose(0, 2, 1, 3).reshape(-1, BLOCK, HD)
+            for x in (past_keys, past_values)
+        ],
+        axis=1,
+    )
+    arrived = lax.all_to_all(stacked[item], "seq", split_axis=0, concat_axis=0, tiled=True)
+    slots = jnp.zeros((8, N), jnp.int32).at[4].set(requests[0])
+    pieces = [(0, 2 * BLOCK)]
+    return attend(queries, span_keys, span_values, slots, pieces, [[arrived]], 0, heads, False)
 
 
 def shards(queries, span_keys, span_values, past_keys, past_values, selected):
@@ -525,28 +550,28 @@
     match = owners[None, :] == jnp.arange(N, dtype=jnp.int32)[:, None]
     outgoing = jnp.sum(jnp.where(match, item[None, :] + 1, 0), axis=1)
     copies = jnp.broadcast_to(outgoing, (N, 1, N))
+    requests = jnp.pad(jnp.stack([owners, item]), ((0, 6), (0, N - owners.shape[0])))
+
+    raw = [swap(past_keys), swap(past_values)]
+    past_keys, past_values, copies = lax.optimization_barrier((past_keys, past_values, copies))
     wanted = lax.all_to_all(copies, "seq", split_axis=0, concat_axis=0, tiled=True).reshape(N, N)
-    requests = jnp.pad(jnp.stack([owners, item]), ((0, 6), (0, N - owners.shape[0])))
-
     own = cut_items(past_keys, past_values)
     ahead = [onward(own[t], t) for t in range(3)]
-    raw = [swap(past_keys), swap(past_values)]
-    raw, wanted = lax.optimization_barrier((raw, wanted))
+    ahead, raw, wanted = lax.optimization_barrier((ahead, raw, wanted))
+    twice = [onward(ahead[t], t) for t in range(3)]
     mate = cut_items(*raw)
-    ahead_mate = [onward(mate[t], t) for t in range(3)]
     table = make_plan(*FAST[:3], place, wanted, requests)
     most = longest(FAST[0], wanted)[:4, 0]
     fits = jnp.all(most <= jnp.array([FAST[1][0], sum(FAST[1]), FAST[2][0], sum(FAST[2])]))
-    ahead, table, fits = lax.optimization_barrier((ahead, table, fits))
-    twice = [onward(ahead[t], t) for t in range(3)]
+    twice, ahead, mate, table, fits = lax.optimization_barrier((twice, ahead, mate, table, fits))
+    ahead_mate = [onward(mate[t], t) for t in range(3)]
+    ahead_mate, twice = lax.optimization_barrier((ahead_mate, twice))
     pools = [
         [own[t], mate[t], ahead[t], ahead_mate[t], swap(ahead[t]), swap(ahead_mate[t]), twice[t], swap(twice[t])]
         for t in range(3)
     ]
-    args = (queries, span_keys, span_values, pools, place, wanted, requests, table)
-    return lax.cond(
-        fits, functools.partial(route, *FAST), functools.partial(route, *SAFE), *args
-    )
+    args = (queries, span_keys, span_values, past_keys, past_values, pools, place, wanted, requests, table)
+    return lax.cond(fits, functools.partial(route, *FAST), dense, *args)
 
 
 def solution(mesh):

time: 521 us -> 479 us (0.919); the launches traced: 512 us -> 478 us
  waiting for transfers between devices: 221 us -> 188 us
  blocking collectives: 0 us -> 18.8 us
  starting transfers between devices: 71.8 us -> 63.4 us
  loops' own time: 9.03 us -> 0.77 us
    ppermute x27, waiting for transfers between devices: 192 us -> 156 us  [onward(): return lax.ppermute(x, 'seq', ring_pairs(axis))]
    all_to_all x0 -> x1, blocking collectives: none -> 18.8 us  [shards(): lax.all_to_all(copies, 'seq', split_axis=0, concat_axis=0, tiled=True)]
    ppermute x23, starting transfers between devices: 39.9 us -> 22.6 us  [swap(): return lax.ppermute(x, 'seq', [(i, i ^ 1) for i in range(N)])]
    ppermute x23, waiting for transfers between devices: 17.5 us -> 32.4 us  [swap(): return lax.ppermute(x, 'seq', [(i, i ^ 1) for i in range(N)])]
    ppermute x27, starting transfers between devices: 26.5 us -> 40.8 us  [onward(): return lax.ppermute(x, 'seq', ring_pairs(axis))]
    all_to_all x1 -> x0, waiting for transfers between devices: 11.9 us -> none  [shards(): lax.all_to_all(copies, 'seq', split_axis=0, concat_axis=0, tiled=True)]
    another operation x1, loops' own time: 9.03 us -> 0.77 us  [shards(): return lax.cond(fits, functools.partial(route, *FAST), dense, *args)]
    all_to_all x1 -> x0, starting transfers between devices: 5.4 us -> none  [shards(): lax.all_to_all(copies, 'seq', split_axis=0, concat_axis=0, tiled=True)]
  transfers between devices with their start and end apart: 51 -> 50, of which waited for: 21 -> 22; matrix products, arithmetic and copies ran while one was open for 0% -> 1% of each run, Pallas kernels for 13% -> 16%
where the time goes in v3:
time: 479 us; the launch traced here: 478 us
  Pallas kernels  193 us (40%)
  waiting for transfers between devices  188 us (39%)
  starting transfers between devices  63.4 us (13%)
  blocking collectives  18.8 us (4%)
  local copies, waits for them, and re-layouts  11 us (2%)
    ppermute x27, waiting for transfers between devices, onward(): return lax.ppermute(x, 'seq', ring_pairs(axis))  156 us
    pallas_call x1, Pallas kernels, attend(): pl.pallas_call(functools.partial(attend_kernel, pieces, counts, (heads, f...  116 us
    pallas_call x12, Pallas kernels, pack(): pl.pallas_call(functools.partial(pack_kernel, row, first, count, len(sour...  63 us
    ppermute x27, starting transfers between devices, onward(): return lax.ppermute(x, 'seq', ring_pairs(axis))  40.8 us
    ppermute x23, waiting for transfers between devices, swap(): return lax.ppermute(x, 'seq', [(i, i ^ 1) for i in range(N)])  32.4 us
    ppermute x23, starting transfers between devices, swap(): return lax.ppermute(x, 'seq', [(i, i ^ 1) for i in range(N)])  22.6 us
    all_to_all x1, blocking collectives, shards(): lax.all_to_all(copies, 'seq', split_axis=0, concat_axis=0, tiled=True)  18.8 us
    pallas_call x2, Pallas kernels, cut_items(): pl.pallas_call(items_kernel, grid=(2, 2), in_specs=[spec, spec], out_spec...  9.61 us
  transfers between devices with their start and end apart: 50, of which 22 were waited for; matrix products, arithmetic and copies ran while one was open for 1% of the time, Pallas kernels for 16%

profile of v3, /device:TPU:1, one launch (start us, length us, event | category | flops | bytes accessed | tf_op | source)
XLA Modules:
  0.0 477.9 jit_solution(12458155230210706218)
XLA Ops:
  2.5 4.6 cut_items.2
  7.2 2.6 collective-permute-start.30
  9.7 3.8 collective-permute-start.31
  13.5 2.7 collective-permute-start.32
  16.2 18.8 %all_to_all.9 = s32[128,1,128]{2,1,0:T(1,128)S(1)} all-to-all(s32[128,1,128]{2,1,0:T(1,128)S(1)} %broadcast_in_dim.33), channel_id=1, replica_groups=mesh['seq'=128] {'seq'}, dimensions={0} | all-to-all | bytes 131072 | tf_op jit(solution)/shard_map/all_to_all | solution.py:557
  40.6 5.0 %cut_items.3 = (bf16[16,352,128]{2,1,0:T(8,128)(2,1)}, bf16[16,336,128]{2,1,0:T(8,128)(2,1)}, bf16[16,336,128]{2,1,0:T(8,128)(2,1)}) custom-call(bf16[2,1,512,1024]{3,2,1,0:T(8,128)(2,1)} %collective-permute-done.33.k_ref, bf16[2,1,512,1024]{3,2,1,0:T(8,128)(2,1)} %collective-permute-done.34.v_ref), custom_call_target="tpu_custom_call" | custom-call | tf_op jit(solution)/shard_map/cut_items/pallas_call | solution.py:204
  45.6 3.5 plan.1
  49.8 4.6 collective-permute-done.36
  59.0 15.3 %collective-permute-done.39 = bf16[16,336,128]{2,1,0:T(8,128)(2,1)S(1)} collective-permute-done((bf16[16,336,128]{2,1,0:T(8,128)(2,1)}, bf16[16,336,128]{2,1,0:T(8,128)(2,1)S(1)}, u32[]{:S(2)}, u32[]{:S(2)}) %collective-permute-start.39) | collective-permute-done | bytes 1376288 | tf_op jit(solution)/shard_map/ppermute | solution.py:479
  74.2 3.9 collective-permute-start.47
  82.9 2.0 collective-permute-done.45
  86.6 2.7 collective-permute-done.46
  89.3 2.0 collective-permute-done.48
  91.3 2.0 collective-permute-done.49
  93.3 384.4 %conditional.1 = (bf16[1024,4096]{1,0:T(8,128)(2,1)}) conditional(s32[]{:T(128)} %convert_element_type.3, (s32[8,128]{1,0:T(8,128)S(1)}, bf16[2,1,512,1024]{3,2,1,0:T(8,128)(2,1)}, bf16[2,1,512,1024]{3,2,1,0:T(8,128)(2,1)}, s32[128,128]{1,0:T(8,128)S(1)}, bf16[1024,4096]{1,0:T(8,128)(2,1)}, /*index=5*/bf16[1024,1024]{1,0:T(8,128)(2,1)}, ...), branch_computations={%region_2.3_spmd, %region_3.4_spmd} | conditional | flops 85907734528 | bytes 775095936 | solution.py:574
  93.3 3.4 pack.12
  96.6 2.3 collective-permute-start
  99.0 3.5 pack.14
  104.2 4.0 pack.13
  108.2 5.5 %pack.17 = bf16[44,336,128]{2,1,0:T(8,128)(2,1)S(1)} custom-call(s32[24,128]{1,0:T(8,128)S(1)} %get-tuple-element.141.table, bf16[16,336,128]{2,1,0:T(8,128)(2,1)S(1)} %copy-done.24, bf16[16,336,128]{2,1,0:T(8,128)(2,1)S(1)} %copy-done.26, bf16[16,336,128]{2,1,0:T(8,128)(2,1)} %get-tuple-element.119.refs_2_.refs_34_, ...), custom_call_target="tpu_custom_call" | custom-call | tf_op jit(solution)/shard_map/cond/branch_1_fun/pack/pallas_call | solution.py:457
  113.7 6.1 %pack.16 = bf16[44,336,128]{2,1,0:T(8,128)(2,1)S(1)} custom-call(s32[24,128]{1,0:T(8,128)S(1)} %get-tuple-element.141.table, bf16[16,336,128]{2,1,0:T(8,128)(2,1)S(1)} %copy-done.23, bf16[16,336,128]{2,1,0:T(8,128)(2,1)S(1)} %copy-done.25, bf16[16,336,128]{2,1,0:T(8,128)(2,1)} %get-tuple-element.111.refs_2_.refs_18_, bf16[16,336,128]{2,1,0:T(8,128)(2,1)S(1)} %copy-done.28, ...), custom_call_target="tpu_custom_call" | custom-call | tf_op jit(solution)/shard_map/cond/branch_1_fun/pack/pallas_call | solution.py:457
  119.8 5.5 %pack.15 = bf16[44,352,128]{2,1,0:T(8,128)(2,1)S(1)} custom-call(s32[24,128]{1,0:T(8,128)S(1)} %get-tuple-element.141.table, bf16[16,352,128]{2,1,0:T(8,128)(2,1)S(1)} %get-tuple-element.101.refs_0_, bf16[16,352,128]{2,1,0:T(8,128)(2,1)S(1)} %copy-done.19, bf16[16,352,128]{2,1,0:T(8,128)(2,1)S(1)} %get-tuple-element.103.refs_2_, ...), custom_call_target="tpu_custom_call" | custom-call | tf_op jit(solution)/shard_map/cond/branch_1_fun/pack/pallas_call | solution.py:457
  125.6 5.3 %collective-permute-done.1 = bf16[22,336,128]{2,1,0:T(8,128)(2,1)S(1)} collective-permute-done((bf16[22,336,128]{2,1,0:T(8,128)(2,1)S(1)}, bf16[22,336,128]{2,1,0:T(8,128)(2,1)S(1)}, u32[]{:S(2)}, u32[]{:S(2)}) %collective-permute-start.1) | collective-permute-done | bytes 1892384 | tf_op jit(solution)/shard_map/cond/branch_1_fun/ppermute | solution.py:479
  134.1 41.8 %collective-permute-done.4.refs_8_.refs_24_ = bf16[44,336,128]{2,1,0:T(8,128)(2,1)S(1)} collective-permute-done((bf16[44,336,128]{2,1,0:T(8,128)(2,1)S(1)}, bf16[44,336,128]{2,1,0:T(8,128)(2,1)S(1)}, u32[]{:S(2)}, u32[]{:S(2)}) %collective-permute-start.4) | collective-permute-done | bytes 3784736 | tf_op jit(solution)/shard_map/cond/branch_1_fun/ppermute | solution.py:479
  180.4 21.5 %collective-permute-done.8.refs_10_.refs_26_ = bf16[22,336,128]{2,1,0:T(8,128)(2,1)S(1)} collective-permute-done((bf16[22,336,128]{2,1,0:T(8,128)(2,1)S(1)}, bf16[22,336,128]{2,1,0:T(8,128)(2,1)S(1)}, u32[]{:S(2)}, u32[]{:S(2)}) %collective-permute-start.8) | collective-permute-done | bytes 1892384 | tf_op jit(solution)/shard_map/cond/branch_1_fun/ppermute | solution.py:479
  204.9 3.1 collective-permute-done.10.refs_11_
  208.4 4.3 pack.18
  212.7 2.6 collective-permute-start.15
  215.3 6.2 %collective-permute-done.12.refs_11_.refs_27_ = bf16[22,336,128]{2,1,0:T(8,128)(2,1)S(1)} collective-permute-done((bf16[22,336,128]{2,1,0:T(8,128)(2,1)S(1)}, bf16[22,336,128]{2,1,0:T(8,128)(2,1)S(1)}, u32[]{:S(2)}, u32[]{:S(2)}) %collective-permute-start.12) | collective-permute-done | bytes 1892384 | tf_op jit(solution)/shard_map/cond/branch_1_fun/ppermute | solution.py:483
  221.5 4.3 pack.19
  227.5 4.2 pack.20
  231.6 2.4 collective-permute-start.17
  234.0 7.2 %pack.23 = bf16[48,336,128]{2,1,0:T(8,128)(2,1)S(1)} custom-call(s32[24,128]{1,0:T(8,128)S(1)} %get-tuple-element.141.table, bf16[16,336,128]{2,1,0:T(8,128)(2,1)S(1)} %copy-done.24, bf16[16,336,128]{2,1,0:T(8,128)(2,1)S(1)} %copy-done.26, bf16[16,336,128]{2,1,0:T(8,128)(2,1)} %get-tuple-element.119.refs_2_.refs_34_, ...), custom_call_target="tpu_custom_call" | custom-call | tf_op jit(solution)/shard_map/cond/branch_1_fun/pack/pallas_call | solution.py:457
  241.3 7.7 %pack.22 = bf16[48,336,128]{2,1,0:T(8,128)(2,1)S(1)} custom-call(s32[24,128]{1,0:T(8,128)S(1)} %get-tuple-element.141.table, bf16[16,336,128]{2,1,0:T(8,128)(2,1)} %get-tuple-element.109.refs_0_.refs_16_, bf16[16,336,128]{2,1,0:T(8,128)(2,1)} %get-tuple-element.110.refs_1_.refs_17_, bf16[16,336,128]{2,1,0:T(8,128)(2,1)} %get-tuple-element.111.refs_2_.refs_18_, ...), custom_call_target="tpu_custom_call" | custom-call | tf_op jit(solution)/shard_map/cond/branch_1_fun/pack/pallas_call | solution.py:457
  249.1 7.5 %pack.21 = bf16[48,352,128]{2,1,0:T(8,128)(2,1)S(1)} custom-call(s32[24,128]{1,0:T(8,128)S(1)} %get-tuple-element.141.table, bf16[16,352,128]{2,1,0:T(8,128)(2,1)S(1)} %get-tuple-element.101.refs_0_, bf16[16,352,128]{2,1,0:T(8,128)(2,1)S(1)} %copy-done.19, bf16[16,352,128]{2,1,0:T(8,128)(2,1)S(1)} %get-tuple-element.103.refs_2_, ...), custom_call_target="tpu_custom_call" | custom-call | tf_op jit(solution)/shard_map/cond/branch_1_fun/pack/pallas_call | solution.py:457
  259.3 2.6 collective-permute-start.20
  261.9 43.2 %collective-permute-done.19.refs_28_ = bf16[48,336,128]{2,1,0:T(8,128)(2,1)S(1)} collective-permute-done((bf16[48,336,128]{2,1,0:T(8,128)(2,1)S(1)}, bf16[48,336,128]{2,1,0:T(8,128)(2,1)S(1)}, u32[]{:S(2)}, u32[]{:S(2)}) %collective-permute-start.19) | collective-permute-done | bytes 4128800 | tf_op jit(solution)/shard_map/cond/branch_1_fun/ppermute | solution.py:479
  307.8 3.0 collective-permute-start.26
  312.9 18.8 %collective-permute-done.23.refs_30_ = bf16[24,336,128]{2,1,0:T(8,128)(2,1)S(1)} collective-permute-done((bf16[24,336,128]{2,1,0:T(8,128)(2,1)}, bf16[24,336,128]{2,1,0:T(8,128)(2,1)S(1)}, u32[]{:S(2)}, u32[]{:S(2)}) %collective-permute-start.23) | collective-permute-done | bytes 2064416 | tf_op jit(solution)/shard_map/cond/branch_1_fun/ppermute | solution.py:479
  331.7 6.2 %collective-permute-start.28 = (bf16[48,336,128]{2,1,0:T(8,128)(2,1)S(1)}, bf16[48,336,128]{2,1,0:T(8,128)(2,1)S(1)}, u32[]{:S(2)}, u32[]{:S(2)}) collective-permute-start(bf16[48,336,128]{2,1,0:T(8,128)(2,1)S(1)} %collective-permute-done.20.refs_44_), channel_id=1, source_target_pairs={{0,1},{1,0},{2,3},{3,2},{4,5},{5,4},{6,7},{7,6},{8,9},{9,8},{10,11... | collective-permute-start | bytes 12386312 | tf_op jit(solution)/shard_map/cond/branch_1_fun/ppermute | solution.py:483
  337.9 2.2 collective-permute-start.25
  340.9 3.7 collective-permute-done.28.refs_45_
  344.6 6.0 %collective-permute-done.27.refs_31_ = bf16[24,336,128]{2,1,0:T(8,128)(2,1)S(1)} collective-permute-done((bf16[24,336,128]{2,1,0:T(8,128)(2,1)S(1)}, bf16[24,336,128]{2,1,0:T(8,128)(2,1)S(1)}, u32[]{:S(2)}, u32[]{:S(2)}) %collective-permute-start.27) | collective-permute-done | bytes 2064416 | tf_op jit(solution)/shard_map/cond/branch_1_fun/ppermute | solution.py:483
  350.6 3.0 collective-permute-done.29.refs_47_
  353.6 2.0 copy-done.42
  355.7 2.1 copy-done.3
  357.8 2.1 copy-done.7
  361.4 116.0 %attend.3 = bf16[1024,4096]{1,0:T(8,128)(2,1)} custom-call(s32[24,128]{1,0:T(8,128)S(1)} %get-tuple-element.141.table, bf16[1024,4096]{1,0:T(8,128)(2,1)} %get-tuple-element.98.q_ref, bf16[1024,1024]{1,0:T(8,128)(2,1)} %get-tuple-element.99.nk_ref, bf16[1024,1024]{1,0:T(8,128)(2,1)} %get-tuple-element.100.nv_ref, ...), custom_call_target="tpu_custom_call" | custom-call | flops 85899345920 | bytes 50331648 | tf_op jit(solution)/shard_map/cond/branch_1_fun/attend/pallas_call | solution.py:152
  (176 shorter events, 43.5 us)
Async XLA Ops:
  0.0 35.1 %collective-permute-start.33 = (bf16[2,1,512,1024]{3,2,1,0:T(8,128)(2,1)}, bf16[2,1,512,1024]{3,2,1,0:T(8,128)(2,1)}, u32[]{:S(2)}, u32[]{:S(2)}) collective-permute-start(bf16[2,1,512,1024]{3,2,1,0:T(8,128)(2,1)} %k_ref), channel_id=1, source_target_pairs={{0,1},{1,0},{2,3},{3,2},{4,5},{5,4},{6,7},{7,6},{8,9},{9,8},{10,11... | collective-permute-start | bytes 6291464 | tf_op jit(solution)/shard_map/ppermute | solution.py:483
  1.4 33.7 %collective-permute-start.34 = (bf16[2,1,512,1024]{3,2,1,0:T(8,128)(2,1)}, bf16[2,1,512,1024]{3,2,1,0:T(8,128)(2,1)}, u32[]{:S(2)}, u32[]{:S(2)}) collective-permute-start(bf16[2,1,512,1024]{3,2,1,0:T(8,128)(2,1)} %v_ref), channel_id=1, source_target_pairs={{0,1},{1,0},{2,3},{3,2},{4,5},{5,4},{6,7},{7,6},{8,9},{9,8},{10,11... | collective-permute-start | bytes 6291464 | tf_op jit(solution)/shard_map/ppermute | solution.py:483
  7.2 27.9 %collective-permute-start.30 = (bf16[16,352,128]{2,1,0:T(8,128)(2,1)S(1)}, bf16[16,352,128]{2,1,0:T(8,128)(2,1)S(1)}, u32[]{:S(2)}, u32[]{:S(2)}) collective-permute-start(bf16[16,352,128]{2,1,0:T(8,128)(2,1)S(1)} %get-tuple-element.191), channel_id=1, source_target_pairs={{0,32},{1,97},{2,34},{3,99},{4,36},{5,101},{6,38},{7,103},{8,40},{... | collective-permute-start | bytes 4325384 | tf_op jit(solution)/shard_map/ppermute | solution.py:479
  9.7 25.3 %collective-permute-start.31 = (bf16[16,336,128]{2,1,0:T(8,128)(2,1)}, bf16[16,336,128]{2,1,0:T(8,128)(2,1)}, u32[]{:S(2)}, u32[]{:S(2)}) collective-permute-start(bf16[16,336,128]{2,1,0:T(8,128)(2,1)} %get-tuple-element.192), channel_id=1, source_target_pairs={{0,8},{1,25},{2,10},{3,27},{4,12},{5,29},{6,14},{7,31},{8,16},{9,1... | collective-permute-start | bytes 4128776 | tf_op jit(solution)/shard_map/ppermute | solution.py:479
  13.5 21.6 %collective-permute-start.32 = (bf16[16,336,128]{2,1,0:T(8,128)(2,1)}, bf16[16,336,128]{2,1,0:T(8,128)(2,1)}, u32[]{:S(2)}, u32[]{:S(2)}) collective-permute-start(bf16[16,336,128]{2,1,0:T(8,128)(2,1)} %get-tuple-element.193), channel_id=1, source_target_pairs={{0,2},{1,7},{2,4},{3,1},{4,6},{5,3},{6,0},{7,5},{8,10},{9,15},{10,... | collective-permute-start | bytes 4128776 | tf_op jit(solution)/shard_map/ppermute | solution.py:479
  35.1 20.1 %collective-permute-start.35 = (bf16[16,352,128]{2,1,0:T(8,128)(2,1)S(1)}, bf16[16,352,128]{2,1,0:T(8,128)(2,1)}, u32[]{:S(2)}, u32[]{:S(2)}) collective-permute-start(bf16[16,352,128]{2,1,0:T(8,128)(2,1)S(1)} %collective-permute-done.30), channel_id=1, source_target_pairs={{0,32},{1,97},{2,34},{3,99},{4,36},{5,101},{6,38},{7,103},{8,40},{... | collective-permute-start | bytes 4325384 | tf_op jit(solution)/shard_map/ppermute | solution.py:479
  36.7 17.8 %collective-permute-start.36 = (bf16[16,336,128]{2,1,0:T(8,128)(2,1)}, bf16[16,336,128]{2,1,0:T(8,128)(2,1)}, u32[]{:S(2)}, u32[]{:S(2)}) collective-permute-start(bf16[16,336,128]{2,1,0:T(8,128)(2,1)} %collective-permute-done.31), channel_id=1, source_target_pairs={{0,8},{1,25},{2,10},{3,27},{4,12},{5,29},{6,14},{7,31},{8,16},{9,1... | collective-permute-start | bytes 4128776 | tf_op jit(solution)/shard_map/ppermute | solution.py:479
  37.4 17.8 %collective-permute-start.37 = (bf16[16,336,128]{2,1,0:T(8,128)(2,1)}, bf16[16,336,128]{2,1,0:T(8,128)(2,1)}, u32[]{:S(2)}, u32[]{:S(2)}) collective-permute-start(bf16[16,336,128]{2,1,0:T(8,128)(2,1)} %collective-permute-done.32), channel_id=1, source_target_pairs={{0,2},{1,7},{2,4},{3,1},{4,6},{5,3},{6,0},{7,5},{8,10},{9,15},{10,... | collective-permute-start | bytes 4128776 | tf_op jit(solution)/shard_map/ppermute | solution.py:479
  55.2 23.0 %collective-permute-start.38 = (bf16[16,352,128]{2,1,0:T(8,128)(2,1)}, bf16[16,352,128]{2,1,0:T(8,128)(2,1)}, u32[]{:S(2)}, u32[]{:S(2)}) collective-permute-start(bf16[16,352,128]{2,1,0:T(8,128)(2,1)} %get-tuple-element.206), channel_id=1, source_target_pairs={{0,32},{1,97},{2,34},{3,99},{4,36},{5,101},{6,38},{7,103},{8,40},{... | collective-permute-start | bytes 4325384 | tf_op jit(solution)/shard_map/ppermute | solution.py:479
  56.5 17.8 %collective-permute-start.39 = (bf16[16,336,128]{2,1,0:T(8,128)(2,1)}, bf16[16,336,128]{2,1,0:T(8,128)(2,1)S(1)}, u32[]{:S(2)}, u32[]{:S(2)}) collective-permute-start(bf16[16,336,128]{2,1,0:T(8,128)(2,1)} %get-tuple-element.208), channel_id=1, source_target_pairs={{0,8},{1,25},{2,10},{3,27},{4,12},{5,29},{6,14},{7,31},{8,16},{9,1... | collective-permute-start | bytes 4128776 | tf_op jit(solution)/shard_map/ppermute | solution.py:479
  57.7 20.5 %collective-permute-start.40 = (bf16[16,336,128]{2,1,0:T(8,128)(2,1)}, bf16[16,336,128]{2,1,0:T(8,128)(2,1)}, u32[]{:S(2)}, u32[]{:S(2)}) collective-permute-start(bf16[16,336,128]{2,1,0:T(8,128)(2,1)} %get-tuple-element.209), channel_id=1, source_target_pairs={{0,2},{1,7},{2,4},{3,1},{4,6},{5,3},{6,0},{7,5},{8,10},{9,15},{10,... | collective-permute-start | bytes 4128776 | tf_op jit(solution)/shard_map/ppermute | solution.py:479
  58.1 23.4 %collective-permute-start.41 = (bf16[16,352,128]{2,1,0:T(8,128)(2,1)S(1)}, bf16[16,352,128]{2,1,0:T(8,128)(2,1)S(1)}, u32[]{:S(2)}, u32[]{:S(2)}) collective-permute-start(bf16[16,352,128]{2,1,0:T(8,128)(2,1)S(1)} %collective-permute-done.30), channel_id=1, source_target_pairs={{0,1},{1,0},{2,3},{3,2},{4,5},{5,4},{6,7},{7,6},{8,9},{9,8},{10,11... | collective-permute-start | bytes 4325384 | tf_op jit(solution)/shard_map/ppermute | solution.py:483
  59.0 19.8 %collective-permute-start.44 = (bf16[16,336,128]{2,1,0:T(8,128)(2,1)}, bf16[16,336,128]{2,1,0:T(8,128)(2,1)S(1)}, u32[]{:S(2)}, u32[]{:S(2)}) collective-permute-start(bf16[16,336,128]{2,1,0:T(8,128)(2,1)} %collective-permute-done.31), channel_id=1, source_target_pairs={{0,1},{1,0},{2,3},{3,2},{4,5},{5,4},{6,7},{7,6},{8,9},{9,8},{10,11... | collective-permute-start | bytes 4128776 | tf_op jit(solution)/shard_map/ppermute | solution.py:483
  74.2 6.9 %collective-permute-start.47 = (bf16[16,336,128]{2,1,0:T(8,128)(2,1)}, bf16[16,336,128]{2,1,0:T(8,128)(2,1)S(1)}, u32[]{:S(2)}, u32[]{:S(2)}) collective-permute-start(bf16[16,336,128]{2,1,0:T(8,128)(2,1)} %collective-permute-done.32), channel_id=1, source_target_pairs={{0,1},{1,0},{2,3},{3,2},{4,5},{5,4},{6,7},{7,6},{8,9},{9,8},{10,11... | collective-permute-start | bytes 4128776 | tf_op jit(solution)/shard_map/ppermute | solution.py:483
  78.8 14.5 %collective-permute-start.42 = (bf16[16,352,128]{2,1,0:T(8,128)(2,1)}, bf16[16,352,128]{2,1,0:T(8,128)(2,1)}, u32[]{:S(2)}, u32[]{:S(2)}) collective-permute-start(bf16[16,352,128]{2,1,0:T(8,128)(2,1)} %collective-permute-done.38), channel_id=1, source_target_pairs={{0,1},{1,0},{2,3},{3,2},{4,5},{5,4},{6,7},{7,6},{8,9},{9,8},{10,11... | collective-permute-start | bytes 4325384 | tf_op jit(solution)/shard_map/ppermute | solution.py:483
  78.8 14.5 %collective-permute-start.43 = (bf16[16,352,128]{2,1,0:T(8,128)(2,1)}, bf16[16,352,128]{2,1,0:T(8,128)(2,1)}, u32[]{:S(2)}, u32[]{:S(2)}) collective-permute-start(bf16[16,352,128]{2,1,0:T(8,128)(2,1)} %collective-permute-done.35), channel_id=1, source_target_pairs={{0,1},{1,0},{2,3},{3,2},{4,5},{5,4},{6,7},{7,6},{8,9},{9,8},{10,11... | collective-permute-start | bytes 4325384 | tf_op jit(solution)/shard_map/ppermute | solution.py:483
  81.1 8.2 %collective-permute-start.46 = (bf16[16,336,128]{2,1,0:T(8,128)(2,1)}, bf16[16,336,128]{2,1,0:T(8,128)(2,1)}, u32[]{:S(2)}, u32[]{:S(2)}) collective-permute-start(bf16[16,336,128]{2,1,0:T(8,128)(2,1)} %collective-permute-done.36), channel_id=1, source_target_pairs={{0,1},{1,0},{2,3},{3,2},{4,5},{5,4},{6,7},{7,6},{8,9},{9,8},{10,11... | collective-permute-start | bytes 4128776 | tf_op jit(solution)/shard_map/ppermute | solution.py:483
  82.7 8.6 %collective-permute-start.48 = (bf16[16,336,128]{2,1,0:T(8,128)(2,1)}, bf16[16,336,128]{2,1,0:T(8,128)(2,1)}, u32[]{:S(2)}, u32[]{:S(2)}) collective-permute-start(bf16[16,336,128]{2,1,0:T(8,128)(2,1)} %collective-permute-done.40), channel_id=1, source_target_pairs={{0,1},{1,0},{2,3},{3,2},{4,5},{5,4},{6,7},{7,6},{8,9},{9,8},{10,11... | collective-permute-start | bytes 4128776 | tf_op jit(solution)/shard_map/ppermute | solution.py:483
  84.9 8.4 %collective-permute-start.49 = (bf16[16,336,128]{2,1,0:T(8,128)(2,1)}, bf16[16,336,128]{2,1,0:T(8,128)(2,1)}, u32[]{:S(2)}, u32[]{:S(2)}) collective-permute-start(bf16[16,336,128]{2,1,0:T(8,128)(2,1)} %collective-permute-done.37), channel_id=1, source_target_pairs={{0,1},{1,0},{2,3},{3,2},{4,5},{5,4},{6,7},{7,6},{8,9},{9,8},{10,11... | collective-permute-start | bytes 4128776 | tf_op jit(solution)/shard_map/ppermute | solution.py:483
  96.6 34.2 %collective-permute-start = (bf16[22,352,128]{2,1,0:T(8,128)(2,1)S(1)}, bf16[22,352,128]{2,1,0:T(8,128)(2,1)S(1)}, u32[]{:S(2)}, u32[]{:S(2)}) collective-permute-start(bf16[22,352,128]{2,1,0:T(8,128)(2,1)S(1)} %pack.12), channel_id=1, source_target_pairs={{0,8},{1,25},{2,10},{3,27},{4,12},{5,29},{6,14},{7,31},{8,16},{9,1... | collective-permute-start | bytes 5947400 | tf_op jit(solution)/shard_map/cond/branch_1_fun/ppermute | solution.py:479
  102.5 23.1 %collective-permute-start.2 = (bf16[22,336,128]{2,1,0:T(8,128)(2,1)S(1)}, bf16[22,336,128]{2,1,0:T(8,128)(2,1)S(1)}, u32[]{:S(2)}, u32[]{:S(2)}) collective-permute-start(bf16[22,336,128]{2,1,0:T(8,128)(2,1)S(1)} %pack.14), channel_id=1, source_target_pairs={{0,32},{1,97},{2,34},{3,99},{4,36},{5,101},{6,38},{7,103},{8,40},{... | collective-permute-start | bytes 5677064 | tf_op jit(solution)/shard_map/cond/branch_1_fun/ppermute | solution.py:479
  108.1 22.8 %collective-permute-start.1 = (bf16[22,336,128]{2,1,0:T(8,128)(2,1)S(1)}, bf16[22,336,128]{2,1,0:T(8,128)(2,1)S(1)}, u32[]{:S(2)}, u32[]{:S(2)}) collective-permute-start(bf16[22,336,128]{2,1,0:T(8,128)(2,1)S(1)} %pack.13), channel_id=1, source_target_pairs={{0,2},{1,7},{2,4},{3,1},{4,6},{5,3},{6,0},{7,5},{8,10},{9,15},{10,... | collective-permute-start | bytes 5677064 | tf_op jit(solution)/shard_map/cond/branch_1_fun/ppermute | solution.py:479
  130.9 46.3 %collective-permute-start.3 = (bf16[44,352,128]{2,1,0:T(8,128)(2,1)S(1)}, bf16[44,352,128]{2,1,0:T(8,128)(2,1)S(1)}, u32[]{:S(2)}, u32[]{:S(2)}) collective-permute-start(bf16[44,352,128]{2,1,0:T(8,128)(2,1)S(1)} %pack.15), channel_id=1, source_target_pairs={{0,8},{1,25},{2,10},{3,27},{4,12},{5,29},{6,14},{7,31},{8,16},{9,1... | collective-permute-start | bytes 11894792 | tf_op jit(solution)/shard_map/cond/branch_1_fun/ppermute | solution.py:479
  132.7 43.3 %collective-permute-start.4 = (bf16[44,336,128]{2,1,0:T(8,128)(2,1)S(1)}, bf16[44,336,128]{2,1,0:T(8,128)(2,1)S(1)}, u32[]{:S(2)}, u32[]{:S(2)}) collective-permute-start(bf16[44,336,128]{2,1,0:T(8,128)(2,1)S(1)} %pack.16), channel_id=1, source_target_pairs={{0,2},{1,7},{2,4},{3,1},{4,6},{5,3},{6,0},{7,5},{8,10},{9,15},{10,... | collective-permute-start | bytes 11354120 | tf_op jit(solution)/shard_map/cond/branch_1_fun/ppermute | solution.py:479
  133.9 43.3 %collective-permute-start.5 = (bf16[44,336,128]{2,1,0:T(8,128)(2,1)S(1)}, bf16[44,336,128]{2,1,0:T(8,128)(2,1)S(1)}, u32[]{:S(2)}, u32[]{:S(2)}) collective-permute-start(bf16[44,336,128]{2,1,0:T(8,128)(2,1)S(1)} %pack.17), channel_id=1, source_target_pairs={{0,32},{1,97},{2,34},{3,99},{4,36},{5,101},{6,38},{7,103},{8,40},{... | collective-permute-start | bytes 11354120 | tf_op jit(solution)/shard_map/cond/branch_1_fun/ppermute | solution.py:479
  177.1 26.1 %collective-permute-start.7 = (bf16[22,352,128]{2,1,0:T(8,128)(2,1)S(1)}, bf16[22,352,128]{2,1,0:T(8,128)(2,1)S(1)}, u32[]{:S(2)}, u32[]{:S(2)}) collective-permute-start(bf16[22,352,128]{2,1,0:T(8,128)(2,1)S(1)} %collective-permute-done), channel_id=1, source_target_pairs={{0,8},{1,25},{2,10},{3,27},{4,12},{5,29},{6,14},{7,31},{8,16},{9,1... | collective-permute-start | bytes 5947400 | tf_op jit(solution)/shard_map/cond/branch_1_fun/ppermute | solution.py:479
  179.0 23.0 %collective-permute-start.8 = (bf16[22,336,128]{2,1,0:T(8,128)(2,1)S(1)}, bf16[22,336,128]{2,1,0:T(8,128)(2,1)S(1)}, u32[]{:S(2)}, u32[]{:S(2)}) collective-permute-start(bf16[22,336,128]{2,1,0:T(8,128)(2,1)S(1)} %collective-permute-done.1), channel_id=1, source_target_pairs={{0,2},{1,7},{2,4},{3,1},{4,6},{5,3},{6,0},{7,5},{8,10},{9,15},{10,... | collective-permute-start | bytes 5677064 | tf_op jit(solution)/shard_map/cond/branch_1_fun/ppermute | solution.py:479
  180.3 23.0 %collective-permute-start.9 = (bf16[22,336,128]{2,1,0:T(8,128)(2,1)S(1)}, bf16[22,336,128]{2,1,0:T(8,128)(2,1)S(1)}, u32[]{:S(2)}, u32[]{:S(2)}) collective-permute-start(bf16[22,336,128]{2,1,0:T(8,128)(2,1)S(1)} %collective-permute-done.2), channel_id=1, source_target_pairs={{0,32},{1,97},{2,34},{3,99},{4,36},{5,101},{6,38},{7,103},{8,40},{... | collective-permute-start | bytes 5677064 | tf_op jit(solution)/shard_map/cond/branch_1_fun/ppermute | solution.py:479
  180.3 28.1 %collective-permute-start.6 = (bf16[44,352,128]{2,1,0:T(8,128)(2,1)S(1)}, bf16[44,352,128]{2,1,0:T(8,128)(2,1)S(1)}, u32[]{:S(2)}, u32[]{:S(2)}) collective-permute-start(bf16[44,352,128]{2,1,0:T(8,128)(2,1)S(1)} %collective-permute-done.3.refs_8_), channel_id=1, source_target_pairs={{0,1},{1,0},{2,3},{3,2},{4,5},{5,4},{6,7},{7,6},{8,9},{9,8},{10,11... | collective-permute-start | bytes 11894792 | tf_op jit(solution)/shard_map/cond/branch_1_fun/ppermute | solution.py:483
  204.3 10.9 %collective-permute-start.11 = (bf16[44,336,128]{2,1,0:T(8,128)(2,1)S(1)}, bf16[44,336,128]{2,1,0:T(8,128)(2,1)S(1)}, u32[]{:S(2)}, u32[]{:S(2)}) collective-permute-start(bf16[44,336,128]{2,1,0:T(8,128)(2,1)S(1)} %collective-permute-done.4.refs_8_.refs_24_), channel_id=1, source_target_pairs={{0,1},{1,0},{2,3},{3,2},{4,5},{5,4},{6,7},{7,6},{8,9},{9,8},{10,11... | collective-permute-start | bytes 11354120 | tf_op jit(solution)/shard_map/cond/branch_1_fun/ppermute | solution.py:483
  204.4 23.1 %collective-permute-start.13 = (bf16[44,336,128]{2,1,0:T(8,128)(2,1)S(1)}, bf16[44,336,128]{2,1,0:T(8,128)(2,1)S(1)}, u32[]{:S(2)}, u32[]{:S(2)}) collective-permute-start(bf16[44,336,128]{2,1,0:T(8,128)(2,1)S(1)} %collective-permute-done.5.refs_8_.refs_40_), channel_id=1, source_target_pairs={{0,1},{1,0},{2,3},{3,2},{4,5},{5,4},{6,7},{7,6},{8,9},{9,8},{10,11... | collective-permute-start | bytes 11354120 | tf_op jit(solution)/shard_map/cond/branch_1_fun/ppermute | solution.py:483
  204.9 16.6 %collective-permute-start.12 = (bf16[22,336,128]{2,1,0:T(8,128)(2,1)S(1)}, bf16[22,336,128]{2,1,0:T(8,128)(2,1)S(1)}, u32[]{:S(2)}, u32[]{:S(2)}) collective-permute-start(bf16[22,336,128]{2,1,0:T(8,128)(2,1)S(1)} %collective-permute-done.8.refs_10_.refs_26_), channel_id=1, source_target_pairs={{0,1},{1,0},{2,3},{3,2},{4,5},{5,4},{6,7},{7,6},{8,9},{9,8},{10,11... | collective-permute-start | bytes 5677064 | tf_op jit(solution)/shard_map/cond/branch_1_fun/ppermute | solution.py:483
  208.0 19.5 %collective-permute-start.14 = (bf16[22,336,128]{2,1,0:T(8,128)(2,1)S(1)}, bf16[22,336,128]{2,1,0:T(8,128)(2,1)S(1)}, u32[]{:S(2)}, u32[]{:S(2)}) collective-permute-start(bf16[22,336,128]{2,1,0:T(8,128)(2,1)S(1)} %collective-permute-done.9.refs_10_.refs_42_), channel_id=1, source_target_pairs={{0,1},{1,0},{2,3},{3,2},{4,5},{5,4},{6,7},{7,6},{8,9},{9,8},{10,11... | collective-permute-start | bytes 5677064 | tf_op jit(solution)/shard_map/cond/branch_1_fun/ppermute | solution.py:483
  212.7 44.0 %collective-permute-start.15 = (bf16[24,352,128]{2,1,0:T(8,128)(2,1)S(1)}, bf16[24,352,128]{2,1,0:T(8,128)(2,1)}, u32[]{:S(2)}, u32[]{:S(2)}) collective-permute-start(bf16[24,352,128]{2,1,0:T(8,128)(2,1)S(1)} %pack.18), channel_id=1, source_target_pairs={{0,2},{1,7},{2,4},{3,1},{4,6},{5,3},{6,0},{7,5},{8,10},{9,15},{10,... | collective-permute-start | bytes 6488072 | tf_op jit(solution)/shard_map/cond/branch_1_fun/ppermute | solution.py:479
  225.8 30.8 %collective-permute-start.16 = (bf16[24,336,128]{2,1,0:T(8,128)(2,1)S(1)}, bf16[24,336,128]{2,1,0:T(8,128)(2,1)}, u32[]{:S(2)}, u32[]{:S(2)}) collective-permute-start(bf16[24,336,128]{2,1,0:T(8,128)(2,1)S(1)} %pack.19), channel_id=1, source_target_pairs={{0,32},{1,97},{2,34},{3,99},{4,36},{5,101},{6,38},{7,103},{8,40},{... | collective-permute-start | bytes 6193160 | tf_op jit(solution)/shard_map/cond/branch_1_fun/ppermute | solution.py:479
  231.6 25.0 %collective-permute-start.17 = (bf16[24,336,128]{2,1,0:T(8,128)(2,1)S(1)}, bf16[24,336,128]{2,1,0:T(8,128)(2,1)}, u32[]{:S(2)}, u32[]{:S(2)}) collective-permute-start(bf16[24,336,128]{2,1,0:T(8,128)(2,1)S(1)} %pack.20), channel_id=1, source_target_pairs={{0,8},{1,25},{2,10},{3,27},{4,12},{5,29},{6,14},{7,31},{8,16},{9,1... | collective-permute-start | bytes 6193160 | tf_op jit(solution)/shard_map/cond/branch_1_fun/ppermute | solution.py:479
  256.6 50.1 %collective-permute-start.18 = (bf16[48,352,128]{2,1,0:T(8,128)(2,1)S(1)}, bf16[48,352,128]{2,1,0:T(8,128)(2,1)S(1)}, u32[]{:S(2)}, u32[]{:S(2)}) collective-permute-start(bf16[48,352,128]{2,1,0:T(8,128)(2,1)S(1)} %pack.21), channel_id=1, source_target_pairs={{0,2},{1,7},{2,4},{3,1},{4,6},{5,3},{6,0},{7,5},{8,10},{9,15},{10,... | collective-permute-start | bytes 12976136 | tf_op jit(solution)/shard_map/cond/branch_1_fun/ppermute | solution.py:479
  258.2 46.9 %collective-permute-start.19 = (bf16[48,336,128]{2,1,0:T(8,128)(2,1)S(1)}, bf16[48,336,128]{2,1,0:T(8,128)(2,1)S(1)}, u32[]{:S(2)}, u32[]{:S(2)}) collective-permute-start(bf16[48,336,128]{2,1,0:T(8,128)(2,1)S(1)} %pack.22), channel_id=1, source_target_pairs={{0,32},{1,97},{2,34},{3,99},{4,36},{5,101},{6,38},{7,103},{8,40},{... | collective-permute-start | bytes 12386312 | tf_op jit(solution)/shard_map/cond/branch_1_fun/ppermute | solution.py:479
  259.3 47.4 %collective-permute-start.20 = (bf16[48,336,128]{2,1,0:T(8,128)(2,1)S(1)}, bf16[48,336,128]{2,1,0:T(8,128)(2,1)S(1)}, u32[]{:S(2)}, u32[]{:S(2)}) collective-permute-start(bf16[48,336,128]{2,1,0:T(8,128)(2,1)S(1)} %pack.23), channel_id=1, source_target_pairs={{0,8},{1,25},{2,10},{3,27},{4,12},{5,29},{6,14},{7,31},{8,16},{9,1... | collective-permute-start | bytes 12386312 | tf_op jit(solution)/shard_map/cond/branch_1_fun/ppermute | solution.py:479
  306.7 25.0 %collective-permute-start.23 = (bf16[24,336,128]{2,1,0:T(8,128)(2,1)}, bf16[24,336,128]{2,1,0:T(8,128)(2,1)S(1)}, u32[]{:S(2)}, u32[]{:S(2)}) collective-permute-start(bf16[24,336,128]{2,1,0:T(8,128)(2,1)} %collective-permute-done.16), channel_id=1, source_target_pairs={{0,32},{1,97},{2,34},{3,99},{4,36},{5,101},{6,38},{7,103},{8,40},{... | collective-permute-start | bytes 6193160 | tf_op jit(solution)/shard_map/cond/branch_1_fun/ppermute | solution.py:479
  307.8 32.3 %collective-permute-start.26 = (bf16[48,336,128]{2,1,0:T(8,128)(2,1)S(1)}, bf16[48,336,128]{2,1,0:T(8,128)(2,1)S(1)}, u32[]{:S(2)}, u32[]{:S(2)}) collective-permute-start(bf16[48,336,128]{2,1,0:T(8,128)(2,1)S(1)} %collective-permute-done.19.refs_28_), channel_id=1, source_target_pairs={{0,1},{1,0},{2,3},{3,2},{4,5},{5,4},{6,7},{7,6},{8,9},{9,8},{10,11... | collective-permute-start | bytes 12386312 | tf_op jit(solution)/shard_map/cond/branch_1_fun/ppermute | solution.py:483
  310.8 27.1 %collective-permute-start.22 = (bf16[24,352,128]{2,1,0:T(8,128)(2,1)}, bf16[24,352,128]{2,1,0:T(8,128)(2,1)S(1)}, u32[]{:S(2)}, u32[]{:S(2)}) collective-permute-start(bf16[24,352,128]{2,1,0:T(8,128)(2,1)} %collective-permute-done.15), channel_id=1, source_target_pairs={{0,2},{1,7},{2,4},{3,1},{4,6},{5,3},{6,0},{7,5},{8,10},{9,15},{10,... | collective-permute-start | bytes 6488072 | tf_op jit(solution)/shard_map/cond/branch_1_fun/ppermute | solution.py:479
  312.5 41.1 %collective-permute-start.21 = (bf16[48,352,128]{2,1,0:T(8,128)(2,1)S(1)}, bf16[48,352,128]{2,1,0:T(8,128)(2,1)S(1)}, u32[]{:S(2)}, u32[]{:S(2)}) collective-permute-start(bf16[48,352,128]{2,1,0:T(8,128)(2,1)S(1)} %collective-permute-done.18.refs_12_), channel_id=1, source_target_pairs={{0,1},{1,0},{2,3},{3,2},{4,5},{5,4},{6,7},{7,6},{8,9},{9,8},{10,11... | collective-permute-start | bytes 12976136 | tf_op jit(solution)/shard_map/cond/branch_1_fun/ppermute | solution.py:483
  312.5 25.5 %collective-permute-start.24 = (bf16[24,336,128]{2,1,0:T(8,128)(2,1)}, bf16[24,336,128]{2,1,0:T(8,128)(2,1)S(1)}, u32[]{:S(2)}, u32[]{:S(2)}) collective-permute-start(bf16[24,336,128]{2,1,0:T(8,128)(2,1)} %collective-permute-done.17), channel_id=1, source_target_pairs={{0,8},{1,25},{2,10},{3,27},{4,12},{5,29},{6,14},{7,31},{8,16},{9,1... | collective-permute-start | bytes 6193160 | tf_op jit(solution)/shard_map/cond/branch_1_fun/ppermute | solution.py:479
  331.7 12.9 %collective-permute-start.28 = (bf16[48,336,128]{2,1,0:T(8,128)(2,1)S(1)}, bf16[48,336,128]{2,1,0:T(8,128)(2,1)S(1)}, u32[]{:S(2)}, u32[]{:S(2)}) collective-permute-start(bf16[48,336,128]{2,1,0:T(8,128)(2,1)S(1)} %collective-permute-done.20.refs_44_), channel_id=1, source_target_pairs={{0,1},{1,0},{2,3},{3,2},{4,5},{5,4},{6,7},{7,6},{8,9},{9,8},{10,11... | collective-permute-start | bytes 12386312 | tf_op jit(solution)/shard_map/cond/branch_1_fun/ppermute | solution.py:483
  337.9 15.7 %collective-permute-start.25 = (bf16[24,352,128]{2,1,0:T(8,128)(2,1)S(1)}, bf16[24,352,128]{2,1,0:T(8,128)(2,1)S(1)}, u32[]{:S(2)}, u32[]{:S(2)}) collective-permute-start(bf16[24,352,128]{2,1,0:T(8,128)(2,1)S(1)} %collective-permute-done.22.refs_14_), channel_id=1, source_target_pairs={{0,1},{1,0},{2,3},{3,2},{4,5},{5,4},{6,7},{7,6},{8,9},{9,8},{10,11... | collective-permute-start | bytes 6488072 | tf_op jit(solution)/shard_map/cond/branch_1_fun/ppermute | solution.py:483
  340.1 10.6 %collective-permute-start.27 = (bf16[24,336,128]{2,1,0:T(8,128)(2,1)S(1)}, bf16[24,336,128]{2,1,0:T(8,128)(2,1)S(1)}, u32[]{:S(2)}, u32[]{:S(2)}) collective-permute-start(bf16[24,336,128]{2,1,0:T(8,128)(2,1)S(1)} %collective-permute-done.23.refs_30_), channel_id=1, source_target_pairs={{0,1},{1,0},{2,3},{3,2},{4,5},{5,4},{6,7},{7,6},{8,9},{9,8},{10,11... | collective-permute-start | bytes 6193160 | tf_op jit(solution)/shard_map/cond/branch_1_fun/ppermute | solution.py:483
  340.1 13.5 %collective-permute-start.29 = (bf16[24,336,128]{2,1,0:T(8,128)(2,1)S(1)}, bf16[24,336,128]{2,1,0:T(8,128)(2,1)S(1)}, u32[]{:S(2)}, u32[]{:S(2)}) collective-permute-start(bf16[24,336,128]{2,1,0:T(8,128)(2,1)S(1)} %collective-permute-done.24.refs_46_), channel_id=1, source_target_pairs={{0,1},{1,0},{2,3},{3,2},{4,5},{5,4},{6,7},{7,6},{8,9},{9,8},{10,11... | collective-permute-start | bytes 6193160 | tf_op jit(solution)/shard_map/cond/branch_1_fun/ppermute | solution.py:483
  (47 other events, 1232.3 us)
